TPU v7x, 32 devices: a whole 2x2x4 slice. The times are simulated.
32 devices in a mesh: fsdp: 8 (over y, x, core), blk: 4 (over z).
Axes of the slice: x: 2, y: 2, z: 4, core: 2. Of those that a mesh axis runs over, the one named last changes fastest.
Arguments:
- grad: bfloat16 [16, 768, 768], P(None, 'fsdp', 'blk'), may hold values from -16 to 16
- owner_slots: int32 [16], replicated, may hold values from 0 to 15, as said below
- stat_left: float32 [16, 768, 768], P('fsdp', None, 'blk'), may hold values from -6 to 6
- stat_right: float32 [16, 768, 768], P('fsdp', None, 'blk'), may hold values from -6 to 6
- basis_left: bfloat16 [16, 768, 768], P('fsdp'), may hold values from -1 to 1, as said below
- basis_right: bfloat16 [16, 768, 768], P('fsdp'), may hold values from -1 to 1, as said below
- moment: float32 [16, 768, 768], P('fsdp', None, 'blk'), may hold values from -3 to 3
- second: float32 [16, 768, 768], P('fsdp', None, 'blk'), may hold values from 0.01 to 0.1
Outputs:
- update: bfloat16 [16, 768, 768], P(None, 'fsdp', 'blk')
- new_left: float32 [16, 768, 768], P('fsdp', None, 'blk')
- new_right: float32 [16, 768, 768], P('fsdp', None, 'blk')
- new_moment: float32 [16, 768, 768], P('fsdp', None, 'blk')
- new_second: float32 [16, 768, 768], P('fsdp', None, 'blk')
- grad_rms: float32 [], replicated
Inputs may be any that keep to these rules, and one draw needn't show every extreme that they name: Each 768 x 768 block of basis_left is orthogonal up to bfloat16 rounding. Each 768 x 768 block of basis_right is orthogonal up to bfloat16 rounding. owner_slots names every block exactly once.
All inputs are finite; a program needn't handle non-finite values.
Results may differ from a plain program's by a relative error of at most 0.0058.
Values may be sent and summed in bfloat16 or wider, within the bound.
No kernel may reach another device: no remote copies, remote signals or barrier semaphores. Data moves between devices by JAX's collectives and lax.ppermute only.
A program may use at most 64 MiB of HBM per device.

v0:
```python
import jax
import jax.numpy as jnp
from jax import lax
from jax.sharding import PartitionSpec as P


clip_level = 0.5
stat_decay = 0.95
beta_one = 0.9
beta_two = 0.95
epsilon = 1e-08


def dot(a, b, da, db):
    return lax.dot_general(a, b, (((da,), (db,)), ((), ())), preferred_element_type=jnp.float32)


def total_over(value, axes):
    for name in axes:
        size = lax.axis_size(name)
        if size & (size - 1):
            value = lax.psum(value, name)
            continue
        step = 1
        while step < size:
            value = value + lax.ppermute(value, name, [(i, i ^ step) for i in range(size)])
            step *= 2
    return value


def after(value, *earlier):
    return lax.optimization_barrier((value,) + earlier)[0]


def send(value, pairs):
    return lax.ppermute(value, "blk", pairs)


SWAP = [(0, 1), (1, 0), (2, 3), (3, 2)]
MIDDLE = [(1, 2), (2, 1)]
OVER = [(0, 2), (3, 1)]
INWARD = [(0, 1), (3, 2)]
OUTWARD = [(1, 0), (2, 3)]


def moments(turned, basis, factor, moment, second):
    rotated = factor * dot(turned, basis, 1, 0)
    new_moment = beta_one * moment + (1.0 - beta_one) * rotated
    new_second = beta_two * second + (1.0 - beta_two) * rotated * rotated
    scaled = (new_moment / (jnp.sqrt(new_second) + epsilon)).astype(jnp.bfloat16)
    back = dot(scaled, basis, 1, 1).astype(jnp.bfloat16)
    return new_moment, new_second, back


def whole_step(grad, owner_slots, stat_left, stat_right, basis_left, basis_right, moment, second):
    blocks, rows, width = grad.shape
    owners = lax.axis_size("fsdp")
    size = lax.axis_size("blk")
    per = blocks // owners
    order = rows * owners
    place = lax.axis_index("blk")
    line = size == 4
    slots = owner_slots.reshape(owners, per)

    own = []
    for s in range(per):
        sent = grad.at[slots[:, s]].get(mode="promise_in_bounds", unique_indices=True)
        piece = lax.all_to_all(sent, "fsdp", split_axis=0, concat_axis=0, tiled=True)
        own.append(piece.reshape(order, width).T)

    partial_sum = jnp.sum(jnp.square(grad.astype(jnp.float32))).reshape(1, 1)
    total = total_over(partial_sum, ("fsdp", "blk"))[0, 0]
    grad_rms = jnp.sqrt(total / (blocks * order * order))
    factor = jnp.minimum(1.0, clip_level / grad_rms)

    upper = place >= 2
    end = (place == 0) | (place == 3)
    if line:
        near_at = jnp.where(upper, 1, 2)
        ids = [place, place ^ 1, near_at, jnp.where(upper, 0, 3)]
    else:
        ids = [lax.rem(place + k, size) for k in range(size)]

    def rearranged(matrix):
        matrix = jnp.concatenate([lax.dynamic_slice_in_dim(matrix, i * width, width, 0) for i in ids], axis=0)
        return jnp.concatenate([lax.dynamic_slice_in_dim(matrix, i * width, width, 1) for i in ids], axis=1)

    turn = []
    for s in range(per):
        turn.append(rearranged(basis_right[s]))

    def canonical(parts):
        if line:
            a, b, c, d = parts
            low = jnp.where(place == 0, a, b), jnp.where(place == 0, b, a)
            high = jnp.where(place == 2, a, b), jnp.where(place == 2, b, a)
            return [
                jnp.where(upper, d, low[0]),
                jnp.where(upper, c, low[1]),
                jnp.where(upper, high[0], c),
                jnp.where(upper, high[1], d),
            ]
        return [sum(jnp.where(i == k, p, 0) for i, p in zip(ids, parts)) for k in range(len(parts))]

    gathered = []
    if line:
        held = None
        for s in range(per):
            pair = send(own[s], SWAP)
            block = own[s] if held is None else after(own[s], *held)
            near = send(block, MIDDLE)
            far = send(block, OVER)
            held = (near, far)
            passed = send(jnp.stack([near, far]), OUTWARD)
            near, far = jnp.where(end, passed[0], near), jnp.where(end, passed[1], far)
            gathered.append([own[s], pair, near, far])
    else:
        for s in range(per):
            every = lax.all_gather(own[s], "blk")
            gathered.append([lax.dynamic_index_in_dim(every, i, 0, keepdims=False) for i in ids])

    lefts, rights, moms, secs = [], [], [], []
    placed = jnp.zeros_like(grad)
    for s in range(per):
        columns = jnp.concatenate(gathered[s], axis=0)
        turned = dot(turn[s][:, :width], columns, 0, 0).astype(jnp.bfloat16)
        new_moment, new_second, back = moments(turned, basis_left[s], factor, moment[s].T, second[s].T)
        moms.append(new_moment.T)
        secs.append(new_second.T)
        if line:
            near = send(back, MIDDLE)
            far = send(back, OVER)
            pair = send(back, INWARD)
            backs = jnp.concatenate([back, pair, near, far], axis=0)
            outer_step = dot(backs, turn[s][width : 2 * width], 0, 1).astype(jnp.bfloat16)
            handed = send(outer_step, OUTWARD)
            step = dot(backs, turn[s][:width], 0, 1).astype(jnp.bfloat16)
            step = jnp.where(end, handed, step)
        else:
            every = lax.all_gather(back, "blk")
            backs = jnp.concatenate([lax.dynamic_index_in_dim(every, i, 0, keepdims=False) for i in ids], axis=0)
            step = dot(backs, turn[s][:width], 0, 1).astype(jnp.bfloat16)
        step = step.reshape(owners, rows, width)
        returned = lax.all_to_all(step, "fsdp", split_axis=0, concat_axis=0, tiled=True)
        placed = placed.at[slots[:, s]].set(returned, unique_indices=True, mode="promise_in_bounds")

        own_rows = lax.dynamic_slice_in_dim(columns, place * width, width, 1)
        outer_left = dot(own_rows, columns, 0, 0)
        outer_right = jnp.concatenate(canonical([dot(own[s], g, 1, 1) for g in gathered[s]]), axis=1)
        weight = (1.0 - stat_decay) * (factor * factor)
        lefts.append((stat_decay * stat_left[s].T + weight * outer_left).T)
        rights.append((stat_decay * stat_right[s].T + weight * outer_right).T)

    return (placed, jnp.stack(lefts), jnp.stack(rights), jnp.stack(moms), jnp.stack(secs), grad_rms)


def solution(mesh):
    split = P("fsdp", None, "blk")
    whole = P("fsdp", None, None)
    return jax.shard_map(
        whole_step,
        mesh=mesh,
        in_specs=(P(None, "fsdp", "blk"), P(), split, split, whole, whole, split, split),
        out_specs=(P(None, "fsdp", "blk"), split, split, split, split, P()),
        check_vma=False,
    )
```

profile of v0, /device:TPU:0, one launch (start us, length us, event | category | flops | bytes accessed | tf_op | source)
XLA Modules:
  0.0 163.0 jit_solution(17700766707652656225)
XLA Ops:
  0.6 2.1 %multiply_reduce_fusion = f32[]{:T(128)} fusion(bf16[16,96,192]{2,1,0:T(8,128)(2,1)} %param.8), kind=kLoop, calls=%fused_computation.4 | loop fusion | flops 884735 | bytes 589828 | tf_op jit(solution)/shard_map/reduce_sum | solution.py:71
  4.2 2.5 %gather_fusion = bf16[8,96,192]{2,1,0:T(8,128)(2,1)} fusion(bf16[16,96,192]{2,1,0:T(8,128)(2,1)} %param.8, s32[1024]{0:T(1024)S(1)} %pad_clamp_fusion.1), kind=kCustom, calls=%fused_computation | custom fusion | bytes 589856 | tf_op jit(solution)/shard_map/gather | solution.py:67
  6.6 4.8 %all-to-all-start = ((bf16[8,96,192]{2,1,0:T(8,128)(2,1)}), bf16[8,96,192]{2,1,0:T(8,128)(2,1)S(1)}, u32[]{:S(2)}, u32[]{:S(2)}) async-start(bf16[8,96,192]{2,1,0:T(8,128)(2,1)} %gather_fusion), calls=%async_computation | async-start | bytes 786432 | tf_op jit(solution)/shard_map/all_to_all | solution.py:68
  11.5 1.9 %fusion.86 = (bf16[1,768,768]{2,1,0:T(8,128)(2,1)S(1)}, bf16[1,768,768]{2,1,0:T(8,128)(2,1)S(1)}) fusion(bf16[2,768,768]{2,1,0:T(8,128)(2,1)} %param.13), kind=kLoop, calls=%fused_computation.169 | loop fusion | bytes 4718592 | tf_op jit(solution)/shard_map/slice | solution.py:90
  15.7 1.9 %constant_dynamic-slice_fusion.7 = (bf16[768,192]{1,0:T(8,128)(2,1)}, bf16[768,192]{1,0:T(8,128)(2,1)}, bf16[768,192]{1,0:T(8,128)(2,1)}, bf16[768,192]{1,0:T(8,128)(2,1)}) fusion(bf16[768,768]{1,0:T(8,128)(2,1)S(1)} %pad_maximum_fusion, s32[]{:T(128)S(6)} %select_n.149, s32[]{:T(128)S(6)} %select_n.154, s32[]{:T(128)S(6)} %select_n.152, s32[]{:T(128)S(6)} %select_n.150), kind=kLoop, calls=%fused_computation.150 | loop fusion | bytes 2359312 | tf_op jit(solution)/shard_map/dynamic_slice | solution.py:86
  17.6 2.2 %all-to-all-done = bf16[8,96,192]{2,1,0:T(8,128)(2,1)S(1)} async-done(((bf16[8,96,192]{2,1,0:T(8,128)(2,1)}), bf16[8,96,192]{2,1,0:T(8,128)(2,1)S(1)}, u32[]{:S(2)}, u32[]{:S(2)}) %all-to-all-start) | async-done | bytes 294944 | tf_op jit(solution)/shard_map/all_to_all | solution.py:68
  19.8 3.5 %all-to-all-start.2 = ((bf16[8,96,192]{2,1,0:T(8,128)(2,1)}), bf16[8,96,192]{2,1,0:T(8,128)(2,1)S(1)}, u32[]{:S(2)}, u32[]{:S(2)}) async-start(bf16[8,96,192]{2,1,0:T(8,128)(2,1)} %gather_fusion.1), calls=%async_computation.2 | async-start | bytes 786432 | tf_op jit(solution)/shard_map/all_to_all | solution.py:68
  23.3 1.9 %constant_dynamic-slice_fusion.3 = (bf16[768,192]{1,0:T(8,128)(2,1)}, bf16[768,192]{1,0:T(8,128)(2,1)}, bf16[768,192]{1,0:T(8,128)(2,1)}, bf16[768,192]{1,0:T(8,128)(2,1)}) fusion(bf16[768,768]{1,0:T(8,128)(2,1)S(1)} %pad_maximum_fusion.3, s32[]{:T(128)S(6)} %select_n.149, s32[]{:T(128)S(6)} %select_n.154, s32[]{:T(128)S(6)} %select_n.152, s32[]{:T(128)S(6)} %select_n.150), kind=kLoop, calls=%fused_computation.146 | loop fusion | bytes 2359312 | tf_op jit(solution)/shard_map/dynamic_slice | solution.py:86
  26.6 3.3 %collective-permute-start.1 = (f32[1,1]{1,0:T(1,128)}, f32[1,1]{1,0:T(1,128)}, u32[]{:S(2)}, u32[]{:S(2)}) collective-permute-start(f32[1,1]{1,0:T(1,128)} %add.96), channel_id=1, source_target_pairs={{0,8},{4,12},{8,0},{12,4},{16,24},{20,28},{24,16},{28,20},{1,9},{5... | collective-permute-start | bytes 20 | tf_op jit(solution)/shard_map/ppermute | solution.py:26
  31.1 2.9 %collective-permute-start.2 = (f32[1,1]{1,0:T(1,128)}, f32[1,1]{1,0:T(1,128)}, u32[]{:S(2)}, u32[]{:S(2)}) collective-permute-start(f32[1,1]{1,0:T(1,128)} %add.97), channel_id=1, source_target_pairs={{0,16},{4,20},{8,24},{12,28},{16,0},{20,4},{24,8},{28,12},{1,17},{... | collective-permute-start | bytes 20 | tf_op jit(solution)/shard_map/ppermute | solution.py:26
  35.4 2.9 %collective-permute-start.3 = (f32[1,1]{1,0:T(1,128)}, f32[1,1]{1,0:T(1,128)}, u32[]{:S(2)}, u32[]{:S(2)}) collective-permute-start(f32[1,1]{1,0:T(1,128)} %add.98), channel_id=1, source_target_pairs={{0,1},{1,0},{2,3},{3,2},{4,5},{5,4},{6,7},{7,6},{8,9},{9,8},{10,11... | collective-permute-start | bytes 20 | tf_op jit(solution)/shard_map/ppermute | solution.py:26
  39.6 4.0 %collective-permute-start.4 = (f32[1,1]{1,0:T(1,128)}, f32[1,1]{1,0:T(1,128)}, u32[]{:S(2)}, u32[]{:S(2)}) collective-permute-start(f32[1,1]{1,0:T(1,128)} %add.99), channel_id=1, source_target_pairs={{0,2},{1,3},{2,0},{3,1},{4,6},{5,7},{6,4},{7,5},{8,10},{9,11},{10,... | collective-permute-start | bytes 20 | tf_op jit(solution)/shard_map/ppermute | solution.py:26
  45.6 6.2 %collective-permute-start.7 = (bf16[192,768]{1,0:T(8,128)(2,1)S(1)}, bf16[192,768]{1,0:T(8,128)(2,1)S(1)}, u32[]{:S(2)}, u32[]{:S(2)}) collective-permute-start(bf16[192,768]{1,0:T(8,128)(2,1)S(1)} %bitcast.174), channel_id=1, source_target_pairs={{0,2},{3,1},{4,6},{7,5},{8,10},{11,9},{12,14},{15,13},{16,18},{19,... | collective-permute-start | bytes 884744 | tf_op jit(solution)/shard_map/ppermute | solution.py:36
  52.1 2.1 %collective-permute-start.13 = (bf16[192,768]{1,0:T(8,128)(2,1)S(1)}, bf16[192,768]{1,0:T(8,128)(2,1)S(1)}, u32[]{:S(2)}, u32[]{:S(2)}) collective-permute-start(bf16[192,768]{1,0:T(8,128)(2,1)S(1)} %bitcast.168), channel_id=1, source_target_pairs={{0,1},{1,0},{2,3},{3,2},{4,5},{5,4},{6,7},{7,6},{8,9},{9,8},{10,11... | collective-permute-start | bytes 884744 | tf_op jit(solution)/shard_map/ppermute | solution.py:36
  56.1 3.1 %collective-permute-done.7 = bf16[192,768]{1,0:T(8,128)(2,1)S(1)} collective-permute-done((bf16[192,768]{1,0:T(8,128)(2,1)S(1)}, bf16[192,768]{1,0:T(8,128)(2,1)S(1)}, u32[]{:S(2)}, u32[]{:S(2)}) %collective-permute-start.7) | collective-permute-done | bytes 294944 | tf_op jit(solution)/shard_map/ppermute | solution.py:36
  59.9 8.1 %collective-permute-start.15 = (bf16[192,768]{1,0:T(8,128)(2,1)S(1)}, bf16[192,768]{1,0:T(8,128)(2,1)S(1)}, u32[]{:S(2)}, u32[]{:S(2)}) collective-permute-start(bf16[192,768]{1,0:T(8,128)(2,1)S(1)} %bitcast.170), channel_id=1, source_target_pairs={{0,2},{3,1},{4,6},{7,5},{8,10},{11,9},{12,14},{15,13},{16,18},{19,... | collective-permute-start | bytes 884744 | tf_op jit(solution)/shard_map/ppermute | solution.py:36
  71.4 2.2 %collective-permute-done.15 = bf16[192,768]{1,0:T(8,128)(2,1)S(1)} collective-permute-done((bf16[192,768]{1,0:T(8,128)(2,1)S(1)}, bf16[192,768]{1,0:T(8,128)(2,1)S(1)}, u32[]{:S(2)}, u32[]{:S(2)}) %collective-permute-start.15) | collective-permute-done | bytes 294944 | tf_op jit(solution)/shard_map/ppermute | solution.py:36
  75.7 8.5 %collective-permute-done.8 = bf16[2,192,768]{2,1,0:T(8,128)(2,1)S(1)} collective-permute-done((bf16[2,192,768]{2,1,0:T(8,128)(2,1)S(1)}, bf16[2,192,768]{2,1,0:T(8,128)(2,1)S(1)}, u32[]{:S(2)}, u32[]{:S(2)}) %collective-permute-start.8) | collective-permute-done | bytes 589856 | tf_op jit(solution)/shard_map/ppermute | solution.py:36
  84.3 3.1 %convolution_multiply_fusion.3 = f32[192,768]{1,0:T(8,128)} fusion(bf16[768,192]{1,0:T(8,128)(2,1)} %get-tuple-element.28, bf16[2,768,768]{2,1,0:T(8,128)(2,1)} %param.12, f32[]{:T(128)S(6)} %min_shard_map.3, bf16[192,768]{1,0:T(8,128)(2,1)S(1)} %get-tuple-element.47, bf16[192,768]{1,0:T(8,128)(2,1)S(1)} %get-tuple-element.46, ...), kind=kOutput, calls=%fused_computation.8 | convolution fusion | flops 457998336 | bytes 3342340 | tf_op jit(solution)/shard_map/dot_general | solution.py:15
  87.3 2.5 %convolution_convert_fusion.6 = bf16[192,768]{1,0:T(8,128)(2,1)S(1)} fusion(bf16[2,768,768]{2,1,0:T(8,128)(2,1)} %param.12, f32[192,768]{1,0:T(8,128)} %convolution_multiply_fusion.3, f32[2,768,192]{1,2,0:T(8,128)} %param.14, f32[2,768,192]{1,2,0:T(8,128)} %param.15), kind=kOutput, calls=%fused_computation.19 | convolution fusion | flops 228114432 | bytes 3244032 | tf_op jit(solution)/shard_map/dot_general | solution.py:15
  91.8 2.8 %collective-permute-start.9 = (bf16[192,768]{1,0:T(8,128)(2,1)S(1)}, bf16[192,768]{1,0:T(8,128)(2,1)S(1)}, u32[]{:S(2)}, u32[]{:S(2)}) collective-permute-start(bf16[192,768]{1,0:T(8,128)(2,1)S(1)} %convolution_convert_fusion.6), channel_id=1, source_target_pairs={{0,1},{3,2},{4,5},{7,6},{8,9},{11,10},{12,13},{15,14},{16,17},{19,... | collective-permute-start | bytes 884744 | tf_op jit(solution)/shard_map/ppermute | solution.py:36
  96.2 1.4 fusion.1
  104.1 3.2 %convolution_multiply_fusion.2 = f32[192,768]{1,0:T(8,128)} fusion(bf16[768,192]{1,0:T(8,128)(2,1)} %get-tuple-element.20, bf16[2,768,768]{2,1,0:T(8,128)(2,1)} %param.12, f32[]{:T(128)S(6)} %min_shard_map.3, bf16[192,768]{1,0:T(8,128)(2,1)S(1)} %get-tuple-element.45, bf16[192,768]{1,0:T(8,128)(2,1)S(1)} %get-tuple-element.44, ...), kind=kOutput, calls=%fused_computation.7 | convolution fusion | flops 457998336 | bytes 3342340 | tf_op jit(solution)/shard_map/dot_general | solution.py:15
  107.3 2.4 %convolution_convert_fusion.4 = bf16[192,768]{1,0:T(8,128)(2,1)S(1)} fusion(bf16[2,768,768]{2,1,0:T(8,128)(2,1)} %param.12, f32[192,768]{1,0:T(8,128)} %convolution_multiply_fusion.2, f32[2,768,192]{1,2,0:T(8,128)S(1)} %copy-done.11, f32[2,768,192]{1,2,0:T(8,128)} %param.15), kind=kOutput, calls=%fused_computation.17 | convolution fusion | flops 228114432 | bytes 3244032 | tf_op jit(solution)/shard_map/dot_general | solution.py:15
  109.7 6.7 %collective-permute-start.19 = (bf16[192,768]{1,0:T(8,128)(2,1)S(1)}, bf16[192,768]{1,0:T(8,128)(2,1)S(1)}, u32[]{:S(2)}, u32[]{:S(2)}) collective-permute-start(bf16[192,768]{1,0:T(8,128)(2,1)S(1)} %convolution_convert_fusion.4), channel_id=1, source_target_pairs={{0,2},{3,1},{4,6},{7,5},{8,10},{11,9},{12,14},{15,13},{16,18},{19,... | collective-permute-start | bytes 884744 | tf_op jit(solution)/shard_map/ppermute | solution.py:36
  117.2 3.3 %collective-permute-start.17 = (bf16[192,768]{1,0:T(8,128)(2,1)S(1)}, bf16[192,768]{1,0:T(8,128)(2,1)S(1)}, u32[]{:S(2)}, u32[]{:S(2)}) collective-permute-start(bf16[192,768]{1,0:T(8,128)(2,1)S(1)} %convolution_convert_fusion.4), channel_id=1, source_target_pairs={{0,1},{3,2},{4,5},{7,6},{8,9},{11,10},{12,13},{15,14},{16,17},{19,... | collective-permute-start | bytes 884744 | tf_op jit(solution)/shard_map/ppermute | solution.py:36
  133.9 4.6 %all-to-all-start.1 = ((bf16[8,96,192]{2,1,0:T(8,128)(2,1)}), bf16[8,96,192]{2,1,0:T(8,128)(2,1)S(1)}, u32[]{:S(2)}, u32[]{:S(2)}) async-start(bf16[8,96,192]{2,1,0:T(8,128)(2,1)} %bitcast.17), calls=%async_computation.1 | async-start | bytes 786432 | tf_op jit(solution)/shard_map/all_to_all | solution.py:144
  138.5 1.8 %convolution_convert_fusion = bf16[768,192]{0,1:T(8,128)(2,1)S(1)} fusion(bf16[768,192]{1,0:T(8,128)(2,1)} %get-tuple-element.21, bf16[768,192]{1,0:T(8,128)(2,1)} %get-tuple-element.22, bf16[768,192]{1,0:T(8,128)(2,1)} %get-tuple-element.23, bf16[768,192]{1,0:T(8,128)(2,1)S(1)} %copy-done.29, bf16[192,768]{1,0:T(8,128)(2,1)} %copy-done.39, ...), kind=kOutput, calls=%fused_computation.13 | convolution fusion | flops 232538112 | bytes 2654208 | tf_op jit(solution)/shard_map/dot_general | solution.py:15
  142.3 4.5 %all-to-all-done.1 = bf16[8,96,192]{2,1,0:T(8,128)(2,1)S(1)} async-done(((bf16[8,96,192]{2,1,0:T(8,128)(2,1)}), bf16[8,96,192]{2,1,0:T(8,128)(2,1)S(1)}, u32[]{:S(2)}, u32[]{:S(2)}) %all-to-all-start.1) | async-done | bytes 294944 | tf_op jit(solution)/shard_map/all_to_all | solution.py:144
  146.8 4.1 %all-to-all-start.3 = ((bf16[8,96,192]{2,1,0:T(8,128)(2,1)}), bf16[8,96,192]{2,1,0:T(8,128)(2,1)}, u32[]{:S(2)}, u32[]{:S(2)}) async-start(bf16[8,96,192]{2,1,0:T(8,128)(2,1)} %bitcast.33), calls=%async_computation.3 | async-start | bytes 786432 | tf_op jit(solution)/shard_map/all_to_all | solution.py:144
  154.1 5.1 %all-to-all-done.3 = bf16[8,96,192]{2,1,0:T(8,128)(2,1)} async-done(((bf16[8,96,192]{2,1,0:T(8,128)(2,1)}), bf16[8,96,192]{2,1,0:T(8,128)(2,1)}, u32[]{:S(2)}, u32[]{:S(2)}) %all-to-all-start.3) | async-done | bytes 294944 | tf_op jit(solution)/shard_map/all_to_all | solution.py:144
  159.3 1.7 %scatter_fusion.1 = bf16[16,96,192]{2,1,0:T(8,128)(2,1)S(1)} fusion(bf16[16,96,192]{2,1,0:T(8,128)(2,1)S(1)} %scatter_fusion, s32[8]{0:T(128)S(1)} %get-tuple-element.8, bf16[8,96,192]{2,1,0:T(8,128)(2,1)} %all-to-all-done.3), kind=kCustom, calls=%fused_computation.3 | custom fusion | bytes 884768 | tf_op jit(solution)/shard_map/scatter | solution.py:145
  (154 shorter events, 45.6 us)
Async XLA Ops:
  2.8 22.5 %collective-permute-start = (f32[1,1]{1,0:T(1,128)}, f32[1,1]{1,0:T(1,128)}, u32[]{:S(2)}, u32[]{:S(2)}) collective-permute-start(f32[1,1]{1,0:T(1,128)} %bitcast.2), channel_id=1, source_target_pairs={{0,4},{4,0},{8,12},{12,8},{16,20},{20,16},{24,28},{28,24},{1,5},{5... | collective-permute-start | bytes 20 | tf_op jit(solution)/shard_map/ppermute | solution.py:26
  6.6 13.1 %all-to-all-start = ((bf16[8,96,192]{2,1,0:T(8,128)(2,1)}), bf16[8,96,192]{2,1,0:T(8,128)(2,1)S(1)}, u32[]{:S(2)}, u32[]{:S(2)}) async-start(bf16[8,96,192]{2,1,0:T(8,128)(2,1)} %gather_fusion), calls=%async_computation | async-start | bytes 786432 | tf_op jit(solution)/shard_map/all_to_all | solution.py:68
  19.8 32.1 %all-to-all-start.2 = ((bf16[8,96,192]{2,1,0:T(8,128)(2,1)}), bf16[8,96,192]{2,1,0:T(8,128)(2,1)S(1)}, u32[]{:S(2)}, u32[]{:S(2)}) async-start(bf16[8,96,192]{2,1,0:T(8,128)(2,1)} %gather_fusion.1), calls=%async_computation.2 | async-start | bytes 786432 | tf_op jit(solution)/shard_map/all_to_all | solution.py:68
  26.6 4.0 %collective-permute-start.1 = (f32[1,1]{1,0:T(1,128)}, f32[1,1]{1,0:T(1,128)}, u32[]{:S(2)}, u32[]{:S(2)}) collective-permute-start(f32[1,1]{1,0:T(1,128)} %add.96), channel_id=1, source_target_pairs={{0,8},{4,12},{8,0},{12,4},{16,24},{20,28},{24,16},{28,20},{1,9},{5... | collective-permute-start | bytes 20 | tf_op jit(solution)/shard_map/ppermute | solution.py:26
  31.1 3.6 %collective-permute-start.2 = (f32[1,1]{1,0:T(1,128)}, f32[1,1]{1,0:T(1,128)}, u32[]{:S(2)}, u32[]{:S(2)}) collective-permute-start(f32[1,1]{1,0:T(1,128)} %add.97), channel_id=1, source_target_pairs={{0,16},{4,20},{8,24},{12,28},{16,0},{20,4},{24,8},{28,12},{1,17},{... | collective-permute-start | bytes 20 | tf_op jit(solution)/shard_map/ppermute | solution.py:26
  35.4 3.6 %collective-permute-start.3 = (f32[1,1]{1,0:T(1,128)}, f32[1,1]{1,0:T(1,128)}, u32[]{:S(2)}, u32[]{:S(2)}) collective-permute-start(f32[1,1]{1,0:T(1,128)} %add.98), channel_id=1, source_target_pairs={{0,1},{1,0},{2,3},{3,2},{4,5},{5,4},{6,7},{7,6},{8,9},{9,8},{10,11... | collective-permute-start | bytes 20 | tf_op jit(solution)/shard_map/ppermute | solution.py:26
  39.6 4.5 %collective-permute-start.4 = (f32[1,1]{1,0:T(1,128)}, f32[1,1]{1,0:T(1,128)}, u32[]{:S(2)}, u32[]{:S(2)}) collective-permute-start(f32[1,1]{1,0:T(1,128)} %add.99), channel_id=1, source_target_pairs={{0,2},{1,3},{2,0},{3,1},{4,6},{5,7},{6,4},{7,5},{8,10},{9,11},{10,... | collective-permute-start | bytes 20 | tf_op jit(solution)/shard_map/ppermute | solution.py:26
  44.9 11.2 %collective-permute-start.6 = (bf16[192,768]{1,0:T(8,128)(2,1)S(1)}, bf16[192,768]{1,0:T(8,128)(2,1)S(1)}, u32[]{:S(2)}, u32[]{:S(2)}) collective-permute-start(bf16[192,768]{1,0:T(8,128)(2,1)S(1)} %bitcast.173), channel_id=1, source_target_pairs={{1,2},{2,1},{5,6},{6,5},{9,10},{10,9},{13,14},{14,13},{17,18},{18,... | collective-permute-start | bytes 884744 | tf_op jit(solution)/shard_map/ppermute | solution.py:36
  45.6 13.6 %collective-permute-start.7 = (bf16[192,768]{1,0:T(8,128)(2,1)S(1)}, bf16[192,768]{1,0:T(8,128)(2,1)S(1)}, u32[]{:S(2)}, u32[]{:S(2)}) collective-permute-start(bf16[192,768]{1,0:T(8,128)(2,1)S(1)} %bitcast.174), channel_id=1, source_target_pairs={{0,2},{3,1},{4,6},{7,5},{8,10},{11,9},{12,14},{15,13},{16,18},{19,... | collective-permute-start | bytes 884744 | tf_op jit(solution)/shard_map/ppermute | solution.py:36
  51.8 17.5 %collective-permute-start.5 = (bf16[192,768]{1,0:T(8,128)(2,1)S(1)}, bf16[192,768]{1,0:T(8,128)(2,1)S(1)}, u32[]{:S(2)}, u32[]{:S(2)}) collective-permute-start(bf16[192,768]{1,0:T(8,128)(2,1)S(1)} %bitcast.175), channel_id=1, source_target_pairs={{0,1},{1,0},{2,3},{3,2},{4,5},{5,4},{6,7},{7,6},{8,9},{9,8},{10,11... | collective-permute-start | bytes 884744 | tf_op jit(solution)/shard_map/ppermute | solution.py:36
  52.1 52.0 %copy-start.9 = (bf16[768,192]{0,1:T(8,128)(2,1)}, bf16[768,192]{0,1:T(8,128)(2,1)S(1)}, u32[]{:S(2)}) copy-start(bf16[768,192]{0,1:T(8,128)(2,1)S(1)} %copy.24) | copy-start | bytes 884740
  52.1 18.3 %collective-permute-start.13 = (bf16[192,768]{1,0:T(8,128)(2,1)S(1)}, bf16[192,768]{1,0:T(8,128)(2,1)S(1)}, u32[]{:S(2)}, u32[]{:S(2)}) collective-permute-start(bf16[192,768]{1,0:T(8,128)(2,1)S(1)} %bitcast.168), channel_id=1, source_target_pairs={{0,1},{1,0},{2,3},{3,2},{4,5},{5,4},{6,7},{7,6},{8,9},{9,8},{10,11... | collective-permute-start | bytes 884744 | tf_op jit(solution)/shard_map/ppermute | solution.py:36
  59.2 12.2 %collective-permute-start.14 = (bf16[192,768]{1,0:T(8,128)(2,1)S(1)}, bf16[192,768]{1,0:T(8,128)(2,1)S(1)}, u32[]{:S(2)}, u32[]{:S(2)}) collective-permute-start(bf16[192,768]{1,0:T(8,128)(2,1)S(1)} %bitcast.169), channel_id=1, source_target_pairs={{1,2},{2,1},{5,6},{6,5},{9,10},{10,9},{13,14},{14,13},{17,18},{18,... | collective-permute-start | bytes 884744 | tf_op jit(solution)/shard_map/ppermute | solution.py:36
  59.9 13.7 %collective-permute-start.15 = (bf16[192,768]{1,0:T(8,128)(2,1)S(1)}, bf16[192,768]{1,0:T(8,128)(2,1)S(1)}, u32[]{:S(2)}, u32[]{:S(2)}) collective-permute-start(bf16[192,768]{1,0:T(8,128)(2,1)S(1)} %bitcast.170), channel_id=1, source_target_pairs={{0,2},{3,1},{4,6},{7,5},{8,10},{11,9},{12,14},{15,13},{16,18},{19,... | collective-permute-start | bytes 884744 | tf_op jit(solution)/shard_map/ppermute | solution.py:36
  68.0 16.1 %collective-permute-start.8 = (bf16[2,192,768]{2,1,0:T(8,128)(2,1)S(1)}, bf16[2,192,768]{2,1,0:T(8,128)(2,1)S(1)}, u32[]{:S(2)}, u32[]{:S(2)}) collective-permute-start(bf16[2,192,768]{2,1,0:T(8,128)(2,1)S(1)} %pad_maximum_fusion.10), channel_id=1, source_target_pairs={{1,0},{2,3},{5,4},{6,7},{9,8},{10,11},{13,12},{14,15},{17,16},{18,... | collective-permute-start | bytes 1769480 | tf_op jit(solution)/shard_map/ppermute | solution.py:36
  70.4 33.7 %copy-start.7 = (bf16[192,768]{1,0:T(8,128)(2,1)}, bf16[192,768]{1,0:T(8,128)(2,1)S(1)}, u32[]{:S(2)}) copy-start(bf16[192,768]{1,0:T(8,128)(2,1)S(1)} %collective-permute-done.13) | copy-start | bytes 884740
  71.4 12.8 %copy-start.18 = (bf16[192,768]{1,0:T(8,128)(2,1)S(1)}, bf16[192,768]{1,0:T(8,128)(2,1)}, u32[]{:S(2)}) copy-start(bf16[192,768]{1,0:T(8,128)(2,1)} %copy-done.17) | copy-start | bytes 884740
  74.4 28.5 %collective-permute-start.16 = (bf16[2,192,768]{2,1,0:T(8,128)(2,1)}, bf16[2,192,768]{2,1,0:T(8,128)(2,1)}, u32[]{:S(2)}, u32[]{:S(2)}) collective-permute-start(bf16[2,192,768]{2,1,0:T(8,128)(2,1)} %pad_maximum_fusion.11), channel_id=1, source_target_pairs={{1,0},{2,3},{5,4},{6,7},{9,8},{10,11},{13,12},{14,15},{17,16},{18,... | collective-permute-start | bytes 1769480 | tf_op jit(solution)/shard_map/ppermute | solution.py:36
  89.8 9.0 %collective-permute-start.11 = (bf16[192,768]{1,0:T(8,128)(2,1)S(1)}, bf16[192,768]{1,0:T(8,128)(2,1)S(1)}, u32[]{:S(2)}, u32[]{:S(2)}) collective-permute-start(bf16[192,768]{1,0:T(8,128)(2,1)S(1)} %convolution_convert_fusion.6), channel_id=1, source_target_pairs={{0,2},{3,1},{4,6},{7,5},{8,10},{11,9},{12,14},{15,13},{16,18},{19,... | collective-permute-start | bytes 884744 | tf_op jit(solution)/shard_map/ppermute | solution.py:36
  91.1 7.7 %collective-permute-start.10 = (bf16[192,768]{1,0:T(8,128)(2,1)S(1)}, bf16[192,768]{1,0:T(8,128)(2,1)S(1)}, u32[]{:S(2)}, u32[]{:S(2)}) collective-permute-start(bf16[192,768]{1,0:T(8,128)(2,1)S(1)} %convolution_convert_fusion.6), channel_id=1, source_target_pairs={{1,2},{2,1},{5,6},{6,5},{9,10},{10,9},{13,14},{14,13},{17,18},{18,... | collective-permute-start | bytes 884744 | tf_op jit(solution)/shard_map/ppermute | solution.py:36
  91.8 7.1 %collective-permute-start.9 = (bf16[192,768]{1,0:T(8,128)(2,1)S(1)}, bf16[192,768]{1,0:T(8,128)(2,1)S(1)}, u32[]{:S(2)}, u32[]{:S(2)}) collective-permute-start(bf16[192,768]{1,0:T(8,128)(2,1)S(1)} %convolution_convert_fusion.6), channel_id=1, source_target_pairs={{0,1},{3,2},{4,5},{7,6},{8,9},{11,10},{12,13},{15,14},{16,17},{19,... | collective-permute-start | bytes 884744 | tf_op jit(solution)/shard_map/ppermute | solution.py:36
  100.5 31.5 %collective-permute-start.12 = (bf16[768,192]{0,1:T(8,128)(2,1)}, bf16[768,192]{0,1:T(8,128)(2,1)}, u32[]{:S(2)}, u32[]{:S(2)}) collective-permute-start(bf16[768,192]{0,1:T(8,128)(2,1)} %convolution_convert_fusion.3), channel_id=1, source_target_pairs={{1,0},{2,3},{5,4},{6,7},{9,8},{10,11},{13,12},{14,15},{17,16},{18,... | collective-permute-start | bytes 884744 | tf_op jit(solution)/shard_map/ppermute | solution.py:36
  107.3 13.5 %copy-start.12 = (f32[2,768,192]{1,2,0:T(8,128)S(1)}, f32[2,768,192]{1,2,0:T(8,128)}, u32[]{:S(2)}) copy-start(f32[2,768,192]{1,2,0:T(8,128)} %param.14) | copy-start | bytes 3538948
  107.3 13.5 %copy-start.13 = (f32[2,768,192]{1,2,0:T(8,128)S(1)}, f32[2,768,192]{1,2,0:T(8,128)}, u32[]{:S(2)}) copy-start(f32[2,768,192]{1,2,0:T(8,128)} %param.15) | copy-start | bytes 3538948
  107.3 13.5 %copy-start.28 = (f32[192,768]{1,0:T(8,128)S(1)}, f32[192,768]{1,0:T(8,128)}, u32[]{:S(2)}) copy-start(f32[192,768]{1,0:T(8,128)} %convolution_multiply_fusion.2) | copy-start | bytes 1769476
  109.7 19.2 %copy-start.38 = (bf16[192,768]{1,0:T(8,128)(2,1)}, bf16[192,768]{1,0:T(8,128)(2,1)S(1)}, u32[]{:S(2)}) copy-start(bf16[192,768]{1,0:T(8,128)(2,1)S(1)} %convolution_convert_fusion.4) | copy-start | bytes 884740
  109.7 19.1 %collective-permute-start.19 = (bf16[192,768]{1,0:T(8,128)(2,1)S(1)}, bf16[192,768]{1,0:T(8,128)(2,1)S(1)}, u32[]{:S(2)}, u32[]{:S(2)}) collective-permute-start(bf16[192,768]{1,0:T(8,128)(2,1)S(1)} %convolution_convert_fusion.4), channel_id=1, source_target_pairs={{0,2},{3,1},{4,6},{7,5},{8,10},{11,9},{12,14},{15,13},{16,18},{19,... | collective-permute-start | bytes 884744 | tf_op jit(solution)/shard_map/ppermute | solution.py:36
  116.5 12.4 %collective-permute-start.18 = (bf16[192,768]{1,0:T(8,128)(2,1)S(1)}, bf16[192,768]{1,0:T(8,128)(2,1)S(1)}, u32[]{:S(2)}, u32[]{:S(2)}) collective-permute-start(bf16[192,768]{1,0:T(8,128)(2,1)S(1)} %convolution_convert_fusion.4), channel_id=1, source_target_pairs={{1,2},{2,1},{5,6},{6,5},{9,10},{10,9},{13,14},{14,13},{17,18},{18,... | collective-permute-start | bytes 884744 | tf_op jit(solution)/shard_map/ppermute | solution.py:36
  117.2 11.7 %collective-permute-start.17 = (bf16[192,768]{1,0:T(8,128)(2,1)S(1)}, bf16[192,768]{1,0:T(8,128)(2,1)S(1)}, u32[]{:S(2)}, u32[]{:S(2)}) collective-permute-start(bf16[192,768]{1,0:T(8,128)(2,1)S(1)} %convolution_convert_fusion.4), channel_id=1, source_target_pairs={{0,1},{3,2},{4,5},{7,6},{8,9},{11,10},{12,13},{15,14},{16,17},{19,... | collective-permute-start | bytes 884744 | tf_op jit(solution)/shard_map/ppermute | solution.py:36
  130.7 9.7 %collective-permute-start.20 = (bf16[768,192]{0,1:T(8,128)(2,1)}, bf16[768,192]{0,1:T(8,128)(2,1)}, u32[]{:S(2)}, u32[]{:S(2)}) collective-permute-start(bf16[768,192]{0,1:T(8,128)(2,1)} %convolution_convert_fusion.1), channel_id=1, source_target_pairs={{1,0},{2,3},{5,4},{6,7},{9,8},{10,11},{13,12},{14,15},{17,16},{18,... | collective-permute-start | bytes 884744 | tf_op jit(solution)/shard_map/ppermute | solution.py:36
  133.9 12.9 %all-to-all-start.1 = ((bf16[8,96,192]{2,1,0:T(8,128)(2,1)}), bf16[8,96,192]{2,1,0:T(8,128)(2,1)S(1)}, u32[]{:S(2)}, u32[]{:S(2)}) async-start(bf16[8,96,192]{2,1,0:T(8,128)(2,1)} %bitcast.17), calls=%async_computation.1 | async-start | bytes 786432 | tf_op jit(solution)/shard_map/all_to_all | solution.py:144
  146.8 12.4 %all-to-all-start.3 = ((bf16[8,96,192]{2,1,0:T(8,128)(2,1)}), bf16[8,96,192]{2,1,0:T(8,128)(2,1)}, u32[]{:S(2)}, u32[]{:S(2)}) async-start(bf16[8,96,192]{2,1,0:T(8,128)(2,1)} %bitcast.33), calls=%async_computation.3 | async-start | bytes 786432 | tf_op jit(solution)/shard_map/all_to_all | solution.py:144
  (35 other events, 87.2 us)
where the time goes:
time: 164 us; the launch traced here: 163 us
  starting transfers between devices  68.9 us (42%)
  waiting for transfers between devices  28.2 us (17%)
  matrix products  24.5 us (15%)
  local copies, waits for them, and re-layouts  23.3 us (14%)
  other arithmetic  11.8 us (7%)
  between operations  6.29 us (4%)
    ppermute x16, starting transfers between devices, send(): return lax.ppermute(value, 'blk', pairs)  38.4 us
    dot_general x18, matrix products, dot(): lax.dot_general(a, b, (((da,), (db,)), ((), ())), preferred_element_type=...  24.5 us
    ppermute x16, waiting for transfers between devices, send(): return lax.ppermute(value, 'blk', pairs)  13.8 us
    ppermute x5, starting transfers between devices, total_over(): lax.ppermute(value, name, [(i, i ^ step) for i in range(size)])  13.6 us
    all_to_all x2, waiting for transfers between devices, whole_step(): lax.all_to_all(step, 'fsdp', split_axis=0, concat_axis=0, tiled=True)  9.66 us
    all_to_all x2, starting transfers between devices, whole_step(): lax.all_to_all(step, 'fsdp', split_axis=0, concat_axis=0, tiled=True)  8.68 us
    all_to_all x2, starting transfers between devices, whole_step(): lax.all_to_all(sent, 'fsdp', split_axis=0, concat_axis=0, tiled=True)  8.27 us
    unnamed x84, local copies, waits for them, and re-layouts  7.34 us
  transfers between devices with their start and end apart: 25, of which 11 were waited for; matrix products, arithmetic and copies ran while one was open for 30% of the time, Pallas kernels for 0%

commit v1 on v0

--- a/solution.py
+++ b/solution.py
@@ -1,6 +1,8 @@
 import jax
 import jax.numpy as jnp
 from jax import lax
+from jax.experimental import pallas as pl
+from jax.experimental.pallas import tpu as pltpu
 from jax.sharding import PartitionSpec as P
 
 
@@ -28,12 +30,59 @@
     return value
 
 
-def after(value, *earlier):
-    return lax.optimization_barrier((value,) + earlier)[0]
-
-
 def send(value, pairs):
     return lax.ppermute(value, "blk", pairs)
+
+
+def take_kernel(slots, grad, send_ref, sum_ref):
+    blocks, rows, width = grad.shape
+    per = blocks // send_ref.shape[0]
+    squares = jnp.zeros((rows, width), jnp.float32)
+    for b in range(blocks):
+        value = grad[b].astype(jnp.float32)
+        squares += value * value
+        send_ref[b // per, pl.ds(b % per * rows, rows), :] = grad[slots[b]]
+    total = jnp.sum(jnp.sum(squares, axis=0, keepdims=True), axis=1, keepdims=True)
+    sum_ref[...] = jnp.broadcast_to(total, sum_ref.shape)
+
+
+def take(grad, owner_slots, owners):
+    blocks, rows, width = grad.shape
+    vmem = pl.BlockSpec(memory_space=pltpu.VMEM)
+    return pl.pallas_call(
+        take_kernel,
+        out_shape=[
+            jax.ShapeDtypeStruct((owners, blocks // owners * rows, width), grad.dtype),
+            jax.ShapeDtypeStruct((owners, 128), jnp.float32),
+        ],
+        in_specs=[pl.BlockSpec(memory_space=pltpu.SMEM), vmem],
+        out_specs=[vmem, vmem],
+        name="take",
+    )(owner_slots, grad)
+
+
+def place_kernel(slots, returned, *rest):
+    placed, sem = rest[-2:]
+    copies = [pltpu.make_async_copy(returned.at[f], placed.at[slots[f]], sem.at[f]) for f in range(returned.shape[0])]
+    for copy in copies:
+        copy.start()
+    for copy in copies:
+        copy.wait()
+
+
+def put(placed, shape, slots, returned):
+    earlier = [] if placed is None else [placed]
+    anywhere = pl.BlockSpec(memory_space=pl.ANY)
+    return pl.pallas_call(
+        place_kernel,
+        out_shape=shape,
+        in_specs=[pl.BlockSpec(memory_space=pltpu.SMEM), anywhere] + [anywhere] * len(earlier),
+        out_specs=anywhere,
+        scratch_shapes=[pltpu.SemaphoreType.DMA((returned.shape[0],))],
+        input_output_aliases={2: 0} if earlier else {},
+        compiler_params=pltpu.CompilerParams(vmem_limit_bytes=1 << 20),
+        name="put",
+    )(slots, returned, *earlier)
 
 
 SWAP = [(0, 1), (1, 0), (2, 3), (3, 2)]
@@ -62,17 +111,6 @@
     line = size == 4
     slots = owner_slots.reshape(owners, per)
 
-    own = []
-    for s in range(per):
-        sent = grad.at[slots[:, s]].get(mode="promise_in_bounds", unique_indices=True)
-        piece = lax.all_to_all(sent, "fsdp", split_axis=0, concat_axis=0, tiled=True)
-        own.append(piece.reshape(order, width).T)
-
-    partial_sum = jnp.sum(jnp.square(grad.astype(jnp.float32))).reshape(1, 1)
-    total = total_over(partial_sum, ("fsdp", "blk"))[0, 0]
-    grad_rms = jnp.sqrt(total / (blocks * order * order))
-    factor = jnp.minimum(1.0, clip_level / grad_rms)
-
     upper = place >= 2
     end = (place == 0) | (place == 3)
     if line:
@@ -88,6 +126,27 @@
     turn = []
     for s in range(per):
         turn.append(rearranged(basis_right[s]))
+
+    own = []
+    if line:
+        sent, total = take(grad, owner_slots, owners)
+        piece = lax.all_to_all(sent, "fsdp", split_axis=0, concat_axis=0, tiled=True)
+        total = total_over(total, ("blk",))
+        piece, total, *turn = lax.optimization_barrier((piece, total, *turn))
+        total = lax.all_to_all(total, "fsdp", split_axis=0, concat_axis=0, tiled=True)
+        total = jnp.sum(total[:, 0])
+        for s in range(per):
+            own.append(piece[:, s * rows : (s + 1) * rows, :width].reshape(order, width).T)
+    else:
+        for s in range(per):
+            piece = grad.at[slots[:, s]].get(mode="promise_in_bounds", unique_indices=True)
+            piece = lax.all_to_all(piece, "fsdp", split_axis=0, concat_axis=0, tiled=True)
+            own.append(piece.reshape(order, width).T)
+
+    if not line:
+        total = total_over(jnp.sum(jnp.square(grad.astype(jnp.float32))).reshape(1, 1), ("fsdp", "blk"))[0, 0]
+    grad_rms = jnp.sqrt(total / (blocks * order * order))
+    factor = jnp.minimum(1.0, clip_level / grad_rms)
 
     def canonical(parts):
         if line:
@@ -104,13 +163,11 @@
 
     gathered = []
     if line:
-        held = None
-        for s in range(per):
-            pair = send(own[s], SWAP)
-            block = own[s] if held is None else after(own[s], *held)
-            near = send(block, MIDDLE)
-            far = send(block, OVER)
-            held = (near, far)
+        pairs = send(jnp.stack(own), SWAP)
+        for s in range(per):
+            pair = pairs[s]
+            near = send(own[s], MIDDLE)
+            far = send(own[s], OVER)
             passed = send(jnp.stack([near, far]), OUTWARD)
             near, far = jnp.where(end, passed[0], near), jnp.where(end, passed[1], far)
             gathered.append([own[s], pair, near, far])
@@ -120,7 +177,7 @@
             gathered.append([lax.dynamic_index_in_dim(every, i, 0, keepdims=False) for i in ids])
 
     lefts, rights, moms, secs = [], [], [], []
-    placed = jnp.zeros_like(grad)
+    placed = None if line else jnp.zeros_like(grad)
     for s in range(per):
         columns = jnp.concatenate(gathered[s], axis=0)
         turned = dot(turn[s][:, :width], columns, 0, 0).astype(jnp.bfloat16)
@@ -142,7 +199,10 @@
             step = dot(backs, turn[s][:width], 0, 1).astype(jnp.bfloat16)
         step = step.reshape(owners, rows, width)
         returned = lax.all_to_all(step, "fsdp", split_axis=0, concat_axis=0, tiled=True)
-        placed = placed.at[slots[:, s]].set(returned, unique_indices=True, mode="promise_in_bounds")
+        if line:
+            placed = put(placed, jax.ShapeDtypeStruct(grad.shape, grad.dtype), slots[:, s], returned)
+        else:
+            placed = placed.at[slots[:, s]].set(returned, unique_indices=True, mode="promise_in_bounds")
 
         own_rows = lax.dynamic_slice_in_dim(columns, place * width, width, 1)
         outer_left = dot(own_rows, columns, 0, 0)

time: 164 us -> 142 us (0.87)
  starting transfers between devices: 68.9 us -> 49.3 us
  local copies, waits for them, and re-layouts: 23.3 us -> 9.73 us
  waiting for transfers between devices: 28.2 us -> 33.9 us
  Pallas kernels: 0 us -> 4.88 us
  other arithmetic: 11.8 us -> 15.2 us
  between operations: 6.29 us -> 3.09 us
    ppermute x16 -> x15, starting transfers between devices: 38.4 us -> 28.8 us  [send(): return lax.ppermute(value, 'blk', pairs)]
    ppermute x5 -> x2, starting transfers between devices: 13.6 us -> 4.3 us  [total_over(): lax.ppermute(value, name, [(i, i ^ step) for i in range(size)])]
    pallas_call x0 -> x3, Pallas kernels: none -> 4.88 us  [the longest x2 2.69 us: put(): pl.pallas_call(place_kernel, out_shape=shape, in_specs=[pl.BlockSpec(memo...]
    unnamed x84 -> x72, local copies, waits for them, and re-layouts: 7.34 us -> 3.09 us
    all_to_all x0 -> x1, starting transfers between devices: none -> 4.02 us  [whole_step(): lax.all_to_all(total, 'fsdp', split_axis=0, concat_axis=0, tiled=True)]
    gather x2 -> x0, local copies, waits for them, and re-layouts: 3.77 us -> none  [whole_step(): grad.at[slots[:, s]].get(mode='promise_in_bounds', unique_indices=True)]
    ppermute x16 -> x15, waiting for transfers between devices: 13.8 us -> 17.6 us  [send(): return lax.ppermute(value, 'blk', pairs)]
    all_to_all x0 -> x1, waiting for transfers between devices: none -> 3.64 us  [whole_step(): lax.all_to_all(total, 'fsdp', split_axis=0, concat_axis=0, tiled=True)]
  transfers between devices with their start and end apart: 25 -> 21, of which waited for: 11 -> 7; matrix products, arithmetic and copies ran while one was open for 30% -> 33% of each run, Pallas kernels for 0% -> 1%
where the time goes in v1:
time: 142 us; the launch traced here: 141 us
  starting transfers between devices  49.3 us (35%)
  waiting for transfers between devices  33.9 us (24%)
  matrix products  24.8 us (17%)
  other arithmetic  15.2 us (11%)
  local copies, waits for them, and re-layouts  9.73 us (7%)
  Pallas kernels  4.88 us (3%)
  between operations  3.09 us (2%)
    ppermute x15, starting transfers between devices, send(): return lax.ppermute(value, 'blk', pairs)  28.8 us
    dot_general x18, matrix products, dot(): lax.dot_general(a, b, (((da,), (db,)), ((), ())), preferred_element_type=...  24.8 us
    ppermute x15, waiting for transfers between devices, send(): return lax.ppermute(value, 'blk', pairs)  17.6 us
    all_to_all x2, waiting for transfers between devices, whole_step(): lax.all_to_all(step, 'fsdp', split_axis=0, concat_axis=0, tiled=True)  10.9 us
    all_to_all x2, starting transfers between devices, whole_step(): lax.all_to_all(step, 'fsdp', split_axis=0, concat_axis=0, tiled=True)  6.91 us
    all_to_all x1, starting transfers between devices, whole_step(): lax.all_to_all(sent, 'fsdp', split_axis=0, concat_axis=0, tiled=True)  5.33 us
    ppermute x2, starting transfers between devices, total_over(): lax.ppermute(value, name, [(i, i ^ step) for i in range(size)])  4.3 us
    all_to_all x1, starting transfers between devices, whole_step(): lax.all_to_all(total, 'fsdp', split_axis=0, concat_axis=0, tiled=True)  4.02 us
  transfers between devices with their start and end apart: 21, of which 7 were waited for; matrix products, arithmetic and copies ran while one was open for 33% of the time, Pallas kernels for 1%

profile of v1, /device:TPU:0, one launch (start us, length us, event | category | flops | bytes accessed | tf_op | source)
XLA Modules:
  0.0 140.9 jit_solution(12934571566519067171)
XLA Ops:
  0.6 2.2 %take.1 = (bf16[8,192,192]{2,1,0:T(8,128)(2,1)}, f32[8,128]{1,0:T(8,128)}) custom-call(s32[16]{0:T(128)} %slots.1, bf16[16,96,192]{2,1,0:T(8,128)(2,1)} %grad.1), custom_call_target="tpu_custom_call" | custom-call | tf_op jit(solution)/shard_map/take/pallas_call | solution.py:52
  2.8 5.3 %all-to-all-start = ((bf16[8,192,192]{2,1,0:T(8,128)(2,1)}), bf16[8,192,192]{2,1,0:T(8,128)(2,1)S(1)}, u32[]{:S(2)}, u32[]{:S(2)}) async-start(bf16[8,192,192]{2,1,0:T(8,128)(2,1)} %get-tuple-element.12), calls=%async_computation | async-start | bytes 1572864 | tf_op jit(solution)/shard_map/all_to_all | solution.py:133
  8.2 1.6 %collective-permute-start = (f32[8,128]{1,0:T(8,128)S(1)}, f32[8,128]{1,0:T(8,128)S(1)}, u32[]{:S(2)}, u32[]{:S(2)}) collective-permute-start(f32[8,128]{1,0:T(8,128)S(1)} %copy-done.30), channel_id=1, source_target_pairs={{0,1},{1,0},{2,3},{3,2},{4,5},{5,4},{6,7},{7,6},{8,9},{9,8},{10,11... | collective-permute-start | bytes 12296 | tf_op jit(solution)/shard_map/ppermute | solution.py:28
  9.8 1.8 %fusion.80 = (bf16[1,768,768]{2,1,0:T(8,128)(2,1)S(1)}, bf16[1,768,768]{2,1,0:T(8,128)(2,1)S(1)}) fusion(bf16[2,768,768]{2,1,0:T(8,128)(2,1)} %param.13), kind=kLoop, calls=%fused_computation.154 | loop fusion | bytes 4718592 | tf_op jit(solution)/shard_map/slice | solution.py:128
  12.6 1.5 %pad_maximum_fusion.3 = bf16[768,768]{1,0:T(8,128)(2,1)} fusion(bf16[768,192]{1,0:T(8,128)(2,1)S(1)} %get-tuple-element.31, bf16[768,192]{1,0:T(8,128)(2,1)S(1)} %get-tuple-element.32, bf16[768,192]{1,0:T(8,128)(2,1)S(1)} %get-tuple-element.33, bf16[768,192]{1,0:T(8,128)(2,1)S(1)} %get-tuple-element.30), kind=kLoop, calls=%fused_computation.19 | loop fusion | flops 4718592 | bytes 2359296 | tf_op jit(solution)/shard_map/concatenate | solution.py:124
  14.9 1.5 %pad_maximum_fusion.1 = bf16[768,768]{1,0:T(8,128)(2,1)} fusion(bf16[768,192]{1,0:T(8,128)(2,1)S(1)} %get-tuple-element.39, bf16[768,192]{1,0:T(8,128)(2,1)S(1)} %get-tuple-element.40, bf16[768,192]{1,0:T(8,128)(2,1)S(1)} %get-tuple-element.41, bf16[768,192]{1,0:T(8,128)(2,1)S(1)} %get-tuple-element.38), kind=kLoop, calls=%fused_computation.17 | loop fusion | flops 4718592 | bytes 2359296 | tf_op jit(solution)/shard_map/concatenate | solution.py:124
  16.6 2.7 %collective-permute-start.1 = (f32[8,128]{1,0:T(8,128)S(1)}, f32[8,128]{1,0:T(8,128)S(1)}, u32[]{:S(2)}, u32[]{:S(2)}) collective-permute-start(f32[8,128]{1,0:T(8,128)S(1)} %add.76), channel_id=1, source_target_pairs={{0,2},{1,3},{2,0},{3,1},{4,6},{5,7},{6,4},{7,5},{8,10},{9,11},{10,... | collective-permute-start | bytes 12296 | tf_op jit(solution)/shard_map/ppermute | solution.py:28
  19.4 1.7 %collective-permute-done.1 = f32[8,128]{1,0:T(8,128)S(1)} collective-permute-done((f32[8,128]{1,0:T(8,128)S(1)}, f32[8,128]{1,0:T(8,128)S(1)}, u32[]{:S(2)}, u32[]{:S(2)}) %collective-permute-start.1) | collective-permute-done | bytes 4128 | tf_op jit(solution)/shard_map/ppermute | solution.py:28
  21.9 5.2 %collective-permute-start.11 = (bf16[192,768]{1,0:T(8,128)(2,1)S(1)}, bf16[192,768]{1,0:T(8,128)(2,1)}, u32[]{:S(2)}, u32[]{:S(2)}) collective-permute-start(bf16[192,768]{1,0:T(8,128)(2,1)S(1)} %bitcast.177), channel_id=1, source_target_pairs={{0,2},{3,1},{4,6},{7,5},{8,10},{11,9},{12,14},{15,13},{16,18},{19,... | collective-permute-start | bytes 884744 | tf_op jit(solution)/shard_map/ppermute | solution.py:34
  27.2 1.4 collective-permute-start.10
  30.6 2.8 %collective-permute-start.4 = (bf16[192,768]{1,0:T(8,128)(2,1)S(1)}, bf16[192,768]{1,0:T(8,128)(2,1)S(1)}, u32[]{:S(2)}, u32[]{:S(2)}) collective-permute-start(bf16[192,768]{1,0:T(8,128)(2,1)S(1)} %bitcast.173), channel_id=1, source_target_pairs={{0,2},{3,1},{4,6},{7,5},{8,10},{11,9},{12,14},{15,13},{16,18},{19,... | collective-permute-start | bytes 884744 | tf_op jit(solution)/shard_map/ppermute | solution.py:34
  34.1 4.0 %all-to-all-start.1 = ((f32[8,1,128]{2,1,0:T(1,128)}), f32[8,1,128]{2,1,0:T(1,128)S(1)}, u32[]{:S(2)}, u32[]{:S(2)}) async-start(f32[8,1,128]{2,1,0:T(1,128)} %bitcast.11), calls=%async_computation.1 | async-start | bytes 8192 | tf_op jit(solution)/shard_map/all_to_all | solution.py:136
  39.1 3.6 %all-to-all-done.1 = f32[8,1,128]{2,1,0:T(1,128)S(1)} async-done(((f32[8,1,128]{2,1,0:T(1,128)}), f32[8,1,128]{2,1,0:T(1,128)S(1)}, u32[]{:S(2)}, u32[]{:S(2)}) %all-to-all-start.1) | async-done | bytes 4128 | tf_op jit(solution)/shard_map/all_to_all | solution.py:136
  46.5 4.7 %collective-permute-done.4 = bf16[192,768]{1,0:T(8,128)(2,1)S(1)} collective-permute-done((bf16[192,768]{1,0:T(8,128)(2,1)S(1)}, bf16[192,768]{1,0:T(8,128)(2,1)S(1)}, u32[]{:S(2)}, u32[]{:S(2)}) %collective-permute-start.4) | collective-permute-done | bytes 294944 | tf_op jit(solution)/shard_map/ppermute | solution.py:34
  56.2 7.1 %collective-permute-done.12 = bf16[2,192,768]{2,1,0:T(8,128)(2,1)S(1)} collective-permute-done((bf16[2,192,768]{2,1,0:T(8,128)(2,1)S(1)}, bf16[2,192,768]{2,1,0:T(8,128)(2,1)S(1)}, u32[]{:S(2)}, u32[]{:S(2)}) %collective-permute-start.12) | collective-permute-done | bytes 589856 | tf_op jit(solution)/shard_map/ppermute | solution.py:34
  63.4 3.2 %convolution_multiply_fusion.2 = f32[192,768]{1,0:T(8,128)} fusion(bf16[2,768,768]{2,1,0:T(8,128)(2,1)} %param.12, bf16[768,768]{1,0:T(8,128)(2,1)} %pad_maximum_fusion.1, f32[]{:T(128)S(6)} %min_shard_map.3, bf16[192,768]{1,0:T(8,128)(2,1)S(1)} %get-tuple-element.59, bf16[192,768]{1,0:T(8,128)(2,1)S(1)} %get-tuple-element.58, ...), kind=kOutput, calls=%fused_computation.2 | convolution fusion | flops 457998336 | bytes 3342340 | tf_op jit(solution)/shard_map/dot_general | solution.py:17
  66.6 3.1 %convolution_convert_fusion.4 = bf16[192,768]{1,0:T(8,128)(2,1)} fusion(bf16[2,768,768]{2,1,0:T(8,128)(2,1)} %param.12, f32[192,768]{1,0:T(8,128)} %convolution_multiply_fusion.2, f32[2,768,192]{1,2,0:T(8,128)S(1)} %copy-done.11, f32[2,768,192]{1,2,0:T(8,128)} %param.15), kind=kOutput, calls=%fused_computation.12 | convolution fusion | flops 228114432 | bytes 3244032 | tf_op jit(solution)/shard_map/dot_general | solution.py:17
  69.7 5.5 %collective-permute-start.15 = (bf16[192,768]{1,0:T(8,128)(2,1)}, bf16[192,768]{1,0:T(8,128)(2,1)}, u32[]{:S(2)}, u32[]{:S(2)}) collective-permute-start(bf16[192,768]{1,0:T(8,128)(2,1)} %convolution_convert_fusion.4), channel_id=1, source_target_pairs={{0,2},{3,1},{4,6},{7,5},{8,10},{11,9},{12,14},{15,13},{16,18},{19,... | collective-permute-start | bytes 884744 | tf_op jit(solution)/shard_map/ppermute | solution.py:34
  75.2 1.4 collective-permute-start.14
  76.5 2.4 %collective-permute-start.13 = (bf16[192,768]{1,0:T(8,128)(2,1)}, bf16[192,768]{1,0:T(8,128)(2,1)}, u32[]{:S(2)}, u32[]{:S(2)}) collective-permute-start(bf16[192,768]{1,0:T(8,128)(2,1)} %convolution_convert_fusion.4), channel_id=1, source_target_pairs={{0,1},{3,2},{4,5},{7,6},{8,9},{11,10},{12,13},{15,14},{16,17},{19,... | collective-permute-start | bytes 884744 | tf_op jit(solution)/shard_map/ppermute | solution.py:34
  82.3 3.3 %convolution_multiply_fusion.3 = f32[192,768]{1,0:T(8,128)} fusion(bf16[2,768,768]{2,1,0:T(8,128)(2,1)} %param.12, bf16[768,768]{1,0:T(8,128)(2,1)} %pad_maximum_fusion.3, f32[]{:T(128)S(6)} %min_shard_map.3, bf16[192,768]{1,0:T(8,128)(2,1)} %copy-done.4, bf16[192,768]{1,0:T(8,128)(2,1)S(1)} %get-tuple-element.60, bf16[192,768]{1,0:T(8,128)(2,1)} %get-tuple-element.57, ...), kind=kOutput, calls=%fused_computation.3 | convolution fusion | flops 457998336 | bytes 3342340 | tf_op jit(solution)/shard_map/dot_general | solution.py:17
  85.7 2.6 %convolution_convert_fusion.6 = bf16[192,768]{1,0:T(8,128)(2,1)S(1)} fusion(bf16[2,768,768]{2,1,0:T(8,128)(2,1)} %param.12, f32[192,768]{1,0:T(8,128)} %convolution_multiply_fusion.3, f32[2,768,192]{1,2,0:T(8,128)} %param.14, f32[2,768,192]{1,2,0:T(8,128)} %param.15), kind=kOutput, calls=%fused_computation.14 | convolution fusion | flops 228114432 | bytes 3244032 | tf_op jit(solution)/shard_map/dot_general | solution.py:17
  88.3 1.4 %collective-permute-start.8 = (bf16[192,768]{1,0:T(8,128)(2,1)S(1)}, bf16[192,768]{1,0:T(8,128)(2,1)S(1)}, u32[]{:S(2)}, u32[]{:S(2)}) collective-permute-start(bf16[192,768]{1,0:T(8,128)(2,1)S(1)} %convolution_convert_fusion.6), channel_id=1, source_target_pairs={{0,2},{3,1},{4,6},{7,5},{8,10},{11,9},{12,14},{15,13},{16,18},{19,... | collective-permute-start | bytes 884744 | tf_op jit(solution)/shard_map/ppermute | solution.py:34
  90.7 1.6 %fusion.31 = (f32[1,768,192]{1,2,0:T(8,128)}, f32[1,768,192]{1,2,0:T(8,128)}, f32[1,768,192]{1,2,0:T(8,128)}, f32[1,768,192]{1,2,0:T(8,128)}) fusion(f32[192,768]{1,0:T(8,128)S(1)} %copy-done.26, f32[2,768,192]{1,2,0:T(8,128)S(1)} %copy-done.12, f32[192,768]{1,0:T(8,128)S(1)} %copy-done.27, f32[2,768,192]{1,2,0:T(8,128)S(1)} %copy-done.13), kind=kLoop, calls=%fused_computation.70 | loop fusion | flops 2064384 | bytes 5898240 | tf_op jit(solution)/shard_map/stack | solution.py:214
  98.0 2.0 %collective-permute-start.6 = (bf16[192,768]{1,0:T(8,128)(2,1)S(1)}, bf16[192,768]{1,0:T(8,128)(2,1)S(1)}, u32[]{:S(2)}, u32[]{:S(2)}) collective-permute-start(bf16[192,768]{1,0:T(8,128)(2,1)S(1)} %convolution_convert_fusion.6), channel_id=1, source_target_pairs={{0,1},{3,2},{4,5},{7,6},{8,9},{11,10},{12,13},{15,14},{16,17},{19,... | collective-permute-start | bytes 884744 | tf_op jit(solution)/shard_map/ppermute | solution.py:34
  101.1 1.7 %convolution_convert_fusion.1 = bf16[768,192]{0,1:T(8,128)(2,1)S(1)} fusion(bf16[768,768]{1,0:T(8,128)(2,1)S(1)} %copy-done.17, bf16[192,768]{1,0:T(8,128)(2,1)} %collective-permute-done.15, bf16[192,768]{1,0:T(8,128)(2,1)} %collective-permute-done.14, bf16[192,768]{1,0:T(8,128)(2,1)} %collective-permute-done.13, bf16[192,768]{1,0:T(8,128)(2,1)} %convolution_convert_fusion.4), kind=kOutput, calls=%fused_computation.9 | convolution fusion | flops 231358464 | bytes 1769472 | tf_op jit(solution)/shard_map/dot_general | solution.py:17
  106.7 1.6 %convolution_convert_fusion = bf16[768,192]{0,1:T(8,128)(2,1)S(1)} fusion(bf16[768,768]{1,0:T(8,128)(2,1)S(1)} %copy-done.17, bf16[192,768]{1,0:T(8,128)(2,1)} %collective-permute-done.15, bf16[192,768]{1,0:T(8,128)(2,1)} %collective-permute-done.14, bf16[192,768]{1,0:T(8,128)(2,1)} %collective-permute-done.13, bf16[192,768]{1,0:T(8,128)(2,1)} %convolution_convert_fusion.4), kind=kOutput, calls=%fused_computation.8 | convolution fusion | flops 231358464 | bytes 1769472 | tf_op jit(solution)/shard_map/dot_general | solution.py:17
  108.3 5.8 %collective-permute-done.16 = bf16[768,192]{0,1:T(8,128)(2,1)S(1)} collective-permute-done((bf16[768,192]{0,1:T(8,128)(2,1)S(1)}, bf16[768,192]{0,1:T(8,128)(2,1)S(1)}, u32[]{:S(2)}, u32[]{:S(2)}) %collective-permute-start.16) | collective-permute-done | bytes 294944 | tf_op jit(solution)/shard_map/ppermute | solution.py:34
  115.0 3.5 %all-to-all-start.3 = ((bf16[8,96,192]{2,1,0:T(8,128)(2,1)}), bf16[8,96,192]{2,1,0:T(8,128)(2,1)S(1)}, u32[]{:S(2)}, u32[]{:S(2)}) async-start(bf16[8,96,192]{2,1,0:T(8,128)(2,1)} %bitcast.38), calls=%async_computation.3 | async-start | bytes 786432 | tf_op jit(solution)/shard_map/all_to_all | solution.py:201
  119.9 6.8 %all-to-all-done.3.returned = bf16[8,96,192]{2,1,0:T(8,128)(2,1)S(1)} async-done(((bf16[8,96,192]{2,1,0:T(8,128)(2,1)}), bf16[8,96,192]{2,1,0:T(8,128)(2,1)S(1)}, u32[]{:S(2)}, u32[]{:S(2)}) %all-to-all-start.3) | async-done | bytes 294944 | tf_op jit(solution)/shard_map/all_to_all | solution.py:201
  126.7 3.5 %all-to-all-start.2 = ((bf16[8,96,192]{2,1,0:T(8,128)(2,1)}), bf16[8,96,192]{2,1,0:T(8,128)(2,1)S(1)}, u32[]{:S(2)}, u32[]{:S(2)}) async-start(bf16[8,96,192]{2,1,0:T(8,128)(2,1)} %bitcast.27), calls=%async_computation.2 | async-start | bytes 786432 | tf_op jit(solution)/shard_map/all_to_all | solution.py:201
  134.3 4.1 %all-to-all-done.2.returned = bf16[8,96,192]{2,1,0:T(8,128)(2,1)S(1)} async-done(((bf16[8,96,192]{2,1,0:T(8,128)(2,1)}), bf16[8,96,192]{2,1,0:T(8,128)(2,1)S(1)}, u32[]{:S(2)}, u32[]{:S(2)}) %all-to-all-start.2) | async-done | bytes 294944 | tf_op jit(solution)/shard_map/all_to_all | solution.py:201
  (137 shorter events, 37.2 us)
Async XLA Ops:
  2.8 5.3 %copy-start.30 = (f32[8,128]{1,0:T(8,128)S(1)}, f32[8,128]{1,0:T(8,128)}, u32[]{:S(2)}) copy-start(f32[8,128]{1,0:T(8,128)} %get-tuple-element.13) | copy-start | bytes 12292
  2.8 18.9 %all-to-all-start = ((bf16[8,192,192]{2,1,0:T(8,128)(2,1)}), bf16[8,192,192]{2,1,0:T(8,128)(2,1)S(1)}, u32[]{:S(2)}, u32[]{:S(2)}) async-start(bf16[8,192,192]{2,1,0:T(8,128)(2,1)} %get-tuple-element.12), calls=%async_computation | async-start | bytes 1572864 | tf_op jit(solution)/shard_map/all_to_all | solution.py:133
  8.2 8.4 %collective-permute-start = (f32[8,128]{1,0:T(8,128)S(1)}, f32[8,128]{1,0:T(8,128)S(1)}, u32[]{:S(2)}, u32[]{:S(2)}) collective-permute-start(f32[8,128]{1,0:T(8,128)S(1)} %copy-done.30), channel_id=1, source_target_pairs={{0,1},{1,0},{2,3},{3,2},{4,5},{5,4},{6,7},{7,6},{8,9},{9,8},{10,11... | collective-permute-start | bytes 12296 | tf_op jit(solution)/shard_map/ppermute | solution.py:28
  16.6 4.6 %collective-permute-start.1 = (f32[8,128]{1,0:T(8,128)S(1)}, f32[8,128]{1,0:T(8,128)S(1)}, u32[]{:S(2)}, u32[]{:S(2)}) collective-permute-start(f32[8,128]{1,0:T(8,128)S(1)} %add.76), channel_id=1, source_target_pairs={{0,2},{1,3},{2,0},{3,1},{4,6},{5,7},{6,4},{7,5},{8,10},{9,11},{10,... | collective-permute-start | bytes 12296 | tf_op jit(solution)/shard_map/ppermute | solution.py:28
  21.9 22.1 %collective-permute-start.11 = (bf16[192,768]{1,0:T(8,128)(2,1)S(1)}, bf16[192,768]{1,0:T(8,128)(2,1)}, u32[]{:S(2)}, u32[]{:S(2)}) collective-permute-start(bf16[192,768]{1,0:T(8,128)(2,1)S(1)} %bitcast.177), channel_id=1, source_target_pairs={{0,2},{3,1},{4,6},{7,5},{8,10},{11,9},{12,14},{15,13},{16,18},{19,... | collective-permute-start | bytes 884744 | tf_op jit(solution)/shard_map/ppermute | solution.py:34
  27.2 16.9 %collective-permute-start.10 = (bf16[192,768]{1,0:T(8,128)(2,1)S(1)}, bf16[192,768]{1,0:T(8,128)(2,1)}, u32[]{:S(2)}, u32[]{:S(2)}) collective-permute-start(bf16[192,768]{1,0:T(8,128)(2,1)S(1)} %bitcast.178), channel_id=1, source_target_pairs={{1,2},{2,1},{5,6},{6,5},{9,10},{10,9},{13,14},{14,13},{17,18},{18,... | collective-permute-start | bytes 884744 | tf_op jit(solution)/shard_map/ppermute | solution.py:34
  28.7 26.7 %copy-start = (bf16[768,192]{0,1:T(8,128)(2,1)}, bf16[768,192]{0,1:T(8,128)(2,1)S(1)}, u32[]{:S(2)}) copy-start(bf16[768,192]{0,1:T(8,128)(2,1)S(1)} %copy.24) | copy-start | bytes 884740
  29.6 23.8 %collective-permute-start.2 = (bf16[2,192,768]{2,1,0:T(8,128)(2,1)}, bf16[2,192,768]{2,1,0:T(8,128)(2,1)S(1)}, u32[]{:S(2)}, u32[]{:S(2)}) collective-permute-start(bf16[2,192,768]{2,1,0:T(8,128)(2,1)} %pad_maximum_fusion.12), channel_id=1, source_target_pairs={{0,1},{1,0},{2,3},{3,2},{4,5},{5,4},{6,7},{7,6},{8,9},{9,8},{10,11... | collective-permute-start | bytes 1769480 | tf_op jit(solution)/shard_map/ppermute | solution.py:34
  30.6 20.6 %collective-permute-start.4 = (bf16[192,768]{1,0:T(8,128)(2,1)S(1)}, bf16[192,768]{1,0:T(8,128)(2,1)S(1)}, u32[]{:S(2)}, u32[]{:S(2)}) collective-permute-start(bf16[192,768]{1,0:T(8,128)(2,1)S(1)} %bitcast.173), channel_id=1, source_target_pairs={{0,2},{3,1},{4,6},{7,5},{8,10},{11,9},{12,14},{15,13},{16,18},{19,... | collective-permute-start | bytes 884744 | tf_op jit(solution)/shard_map/ppermute | solution.py:34
  33.4 17.7 %collective-permute-start.3 = (bf16[192,768]{1,0:T(8,128)(2,1)S(1)}, bf16[192,768]{1,0:T(8,128)(2,1)S(1)}, u32[]{:S(2)}, u32[]{:S(2)}) collective-permute-start(bf16[192,768]{1,0:T(8,128)(2,1)S(1)} %bitcast.174), channel_id=1, source_target_pairs={{1,2},{2,1},{5,6},{6,5},{9,10},{10,9},{13,14},{14,13},{17,18},{18,... | collective-permute-start | bytes 884744 | tf_op jit(solution)/shard_map/ppermute | solution.py:34
  34.1 8.6 %all-to-all-start.1 = ((f32[8,1,128]{2,1,0:T(1,128)}), f32[8,1,128]{2,1,0:T(1,128)S(1)}, u32[]{:S(2)}, u32[]{:S(2)}) async-start(f32[8,1,128]{2,1,0:T(1,128)} %bitcast.11), calls=%async_computation.1 | async-start | bytes 8192 | tf_op jit(solution)/shard_map/all_to_all | solution.py:136
  45.2 18.1 %collective-permute-start.12 = (bf16[2,192,768]{2,1,0:T(8,128)(2,1)S(1)}, bf16[2,192,768]{2,1,0:T(8,128)(2,1)S(1)}, u32[]{:S(2)}, u32[]{:S(2)}) collective-permute-start(bf16[2,192,768]{2,1,0:T(8,128)(2,1)S(1)} %pad_maximum_fusion.14), channel_id=1, source_target_pairs={{1,0},{2,3},{5,4},{6,7},{9,8},{10,11},{13,12},{14,15},{17,16},{18,... | collective-permute-start | bytes 1769480 | tf_op jit(solution)/shard_map/ppermute | solution.py:34
  52.1 27.9 %collective-permute-start.5 = (bf16[2,192,768]{2,1,0:T(8,128)(2,1)}, bf16[2,192,768]{2,1,0:T(8,128)(2,1)}, u32[]{:S(2)}, u32[]{:S(2)}) collective-permute-start(bf16[2,192,768]{2,1,0:T(8,128)(2,1)} %pad_maximum_fusion.13), channel_id=1, source_target_pairs={{1,0},{2,3},{5,4},{6,7},{9,8},{10,11},{13,12},{14,15},{17,16},{18,... | collective-permute-start | bytes 1769480 | tf_op jit(solution)/shard_map/ppermute | solution.py:34
  63.4 15.6 %copy-start.2 = (bf16[192,768]{1,0:T(8,128)(2,1)}, bf16[192,768]{1,0:T(8,128)(2,1)S(1)}, u32[]{:S(2)}) copy-start(bf16[192,768]{1,0:T(8,128)(2,1)S(1)} %get-tuple-element.59) | copy-start | bytes 884740
  69.7 10.4 %copy-start.19 = (bf16[192,768]{1,0:T(8,128)(2,1)S(1)}, bf16[192,768]{1,0:T(8,128)(2,1)}, u32[]{:S(2)}) copy-start(bf16[192,768]{1,0:T(8,128)(2,1)} %copy-done.18) | copy-start | bytes 884740
  69.7 10.4 %copy-start.21 = (bf16[192,768]{1,0:T(8,128)(2,1)S(1)}, bf16[192,768]{1,0:T(8,128)(2,1)}, u32[]{:S(2)}) copy-start(bf16[192,768]{1,0:T(8,128)(2,1)} %copy-done.20) | copy-start | bytes 884740
  69.7 28.3 %collective-permute-start.15 = (bf16[192,768]{1,0:T(8,128)(2,1)}, bf16[192,768]{1,0:T(8,128)(2,1)}, u32[]{:S(2)}, u32[]{:S(2)}) collective-permute-start(bf16[192,768]{1,0:T(8,128)(2,1)} %convolution_convert_fusion.4), channel_id=1, source_target_pairs={{0,2},{3,1},{4,6},{7,5},{8,10},{11,9},{12,14},{15,13},{16,18},{19,... | collective-permute-start | bytes 884744 | tf_op jit(solution)/shard_map/ppermute | solution.py:34
  75.2 26.0 %collective-permute-start.14 = (bf16[192,768]{1,0:T(8,128)(2,1)}, bf16[192,768]{1,0:T(8,128)(2,1)}, u32[]{:S(2)}, u32[]{:S(2)}) collective-permute-start(bf16[192,768]{1,0:T(8,128)(2,1)} %convolution_convert_fusion.4), channel_id=1, source_target_pairs={{1,2},{2,1},{5,6},{6,5},{9,10},{10,9},{13,14},{14,13},{17,18},{18,... | collective-permute-start | bytes 884744 | tf_op jit(solution)/shard_map/ppermute | solution.py:34
  76.5 24.6 %collective-permute-start.13 = (bf16[192,768]{1,0:T(8,128)(2,1)}, bf16[192,768]{1,0:T(8,128)(2,1)}, u32[]{:S(2)}, u32[]{:S(2)}) collective-permute-start(bf16[192,768]{1,0:T(8,128)(2,1)} %convolution_convert_fusion.4), channel_id=1, source_target_pairs={{0,1},{3,2},{4,5},{7,6},{8,9},{11,10},{12,13},{15,14},{16,17},{19,... | collective-permute-start | bytes 884744 | tf_op jit(solution)/shard_map/ppermute | solution.py:34
  85.7 5.0 %copy-start.26 = (f32[192,768]{1,0:T(8,128)S(1)}, f32[192,768]{1,0:T(8,128)}, u32[]{:S(2)}) copy-start(f32[192,768]{1,0:T(8,128)} %convolution_multiply_fusion.2) | copy-start | bytes 1769476
  85.7 5.0 %copy-start.27 = (f32[192,768]{1,0:T(8,128)S(1)}, f32[192,768]{1,0:T(8,128)}, u32[]{:S(2)}) copy-start(f32[192,768]{1,0:T(8,128)} %convolution_multiply_fusion.3) | copy-start | bytes 1769476
  88.3 15.9 %collective-permute-start.8 = (bf16[192,768]{1,0:T(8,128)(2,1)S(1)}, bf16[192,768]{1,0:T(8,128)(2,1)S(1)}, u32[]{:S(2)}, u32[]{:S(2)}) collective-permute-start(bf16[192,768]{1,0:T(8,128)(2,1)S(1)} %convolution_convert_fusion.6), channel_id=1, source_target_pairs={{0,2},{3,1},{4,6},{7,5},{8,10},{11,9},{12,14},{15,13},{16,18},{19,... | collective-permute-start | bytes 884744 | tf_op jit(solution)/shard_map/ppermute | solution.py:34
  89.8 14.4 %collective-permute-start.7 = (bf16[192,768]{1,0:T(8,128)(2,1)S(1)}, bf16[192,768]{1,0:T(8,128)(2,1)S(1)}, u32[]{:S(2)}, u32[]{:S(2)}) collective-permute-start(bf16[192,768]{1,0:T(8,128)(2,1)S(1)} %convolution_convert_fusion.6), channel_id=1, source_target_pairs={{1,2},{2,1},{5,6},{6,5},{9,10},{10,9},{13,14},{14,13},{17,18},{18,... | collective-permute-start | bytes 884744 | tf_op jit(solution)/shard_map/ppermute | solution.py:34
  98.0 6.2 %collective-permute-start.6 = (bf16[192,768]{1,0:T(8,128)(2,1)S(1)}, bf16[192,768]{1,0:T(8,128)(2,1)S(1)}, u32[]{:S(2)}, u32[]{:S(2)}) collective-permute-start(bf16[192,768]{1,0:T(8,128)(2,1)S(1)} %convolution_convert_fusion.6), channel_id=1, source_target_pairs={{0,1},{3,2},{4,5},{7,6},{8,9},{11,10},{12,13},{15,14},{16,17},{19,... | collective-permute-start | bytes 884744 | tf_op jit(solution)/shard_map/ppermute | solution.py:34
  102.9 11.2 %collective-permute-start.16 = (bf16[768,192]{0,1:T(8,128)(2,1)S(1)}, bf16[768,192]{0,1:T(8,128)(2,1)S(1)}, u32[]{:S(2)}, u32[]{:S(2)}) collective-permute-start(bf16[768,192]{0,1:T(8,128)(2,1)S(1)} %convolution_convert_fusion.1), channel_id=1, source_target_pairs={{1,0},{2,3},{5,4},{6,7},{9,8},{10,11},{13,12},{14,15},{17,16},{18,... | collective-permute-start | bytes 884744 | tf_op jit(solution)/shard_map/ppermute | solution.py:34
  105.4 13.6 %collective-permute-start.9 = (bf16[768,192]{0,1:T(8,128)(2,1)}, bf16[768,192]{0,1:T(8,128)(2,1)S(1)}, u32[]{:S(2)}, u32[]{:S(2)}) collective-permute-start(bf16[768,192]{0,1:T(8,128)(2,1)} %convolution_convert_fusion.3), channel_id=1, source_target_pairs={{1,0},{2,3},{5,4},{6,7},{9,8},{10,11},{13,12},{14,15},{17,16},{18,... | collective-permute-start | bytes 884744 | tf_op jit(solution)/shard_map/ppermute | solution.py:34
  108.3 10.2 %copy-start.33 = (bf16[192,768]{1,0:T(8,128)(2,1)S(1)}, bf16[192,768]{1,0:T(8,128)(2,1)}, u32[]{:S(2)}) copy-start(bf16[192,768]{1,0:T(8,128)(2,1)} %copy-done.32) | copy-start | bytes 884740
  108.3 10.2 %copy-start.35 = (bf16[192,768]{1,0:T(8,128)(2,1)S(1)}, bf16[192,768]{1,0:T(8,128)(2,1)}, u32[]{:S(2)}) copy-start(bf16[192,768]{1,0:T(8,128)(2,1)} %copy-done.34) | copy-start | bytes 884740
  115.0 11.7 %all-to-all-start.3 = ((bf16[8,96,192]{2,1,0:T(8,128)(2,1)}), bf16[8,96,192]{2,1,0:T(8,128)(2,1)S(1)}, u32[]{:S(2)}, u32[]{:S(2)}) async-start(bf16[8,96,192]{2,1,0:T(8,128)(2,1)} %bitcast.38), calls=%async_computation.3 | async-start | bytes 786432 | tf_op jit(solution)/shard_map/all_to_all | solution.py:201
  118.9 11.3 %copy-start.8 = (f32[1,768,192]{1,2,0:T(8,128)S(1)}, f32[1,768,192]{1,2,0:T(8,128)}, u32[]{:S(2)}) copy-start(f32[1,768,192]{1,2,0:T(8,128)} %get-tuple-element.24) | copy-start | bytes 1769476
  118.9 11.3 %copy-start.9 = (f32[1,768,192]{1,2,0:T(8,128)S(1)}, f32[1,768,192]{1,2,0:T(8,128)}, u32[]{:S(2)}) copy-start(f32[1,768,192]{1,2,0:T(8,128)} %get-tuple-element.25) | copy-start | bytes 1769476
  126.7 11.7 %all-to-all-start.2 = ((bf16[8,96,192]{2,1,0:T(8,128)(2,1)}), bf16[8,96,192]{2,1,0:T(8,128)(2,1)S(1)}, u32[]{:S(2)}, u32[]{:S(2)}) async-start(bf16[8,96,192]{2,1,0:T(8,128)(2,1)} %bitcast.27), calls=%async_computation.2 | async-start | bytes 786432 | tf_op jit(solution)/shard_map/all_to_all | solution.py:201
  (25 other events, 52.9 us)

commit v2 on v1

--- a/solution.py
+++ b/solution.py
@@ -85,6 +85,58 @@
     )(slots, returned, *earlier)
 
 
+def at_block(index, width):
+    return pl.ds(pl.multiple_of(index * width, width), width)
+
+
+def turn_kernel(ids, own, pair, near, far, passed_near, passed_far, columns, basis, rotated, whole):
+    width = own.shape[0]
+    whole[at_block(ids[0], width), :] = own[...]
+    whole[at_block(ids[1], width), :] = pair[...]
+    whole[at_block(ids[2], width), :] = near[...] + passed_near[...]
+    whole[at_block(ids[3], width), :] = far[...] + passed_far[...]
+    turned = dot(columns[...], whole[...], 0, 0)
+    rotated[...] = dot(turned.astype(jnp.bfloat16), basis[...], 1, 0)
+
+
+def turn_own(ids, blocks, columns, basis):
+    vmem = pl.BlockSpec(memory_space=pltpu.VMEM)
+    return pl.pallas_call(
+        turn_kernel,
+        out_shape=[
+            jax.ShapeDtypeStruct(blocks[0].shape, jnp.float32),
+            jax.ShapeDtypeStruct(basis.shape, blocks[0].dtype),
+        ],
+        in_specs=[pl.BlockSpec(memory_space=pltpu.SMEM)] + [vmem] * 8,
+        out_specs=[vmem, vmem],
+        name="turn_own",
+    )(ids, *blocks, columns, basis)
+
+
+def update_kernel(ids, back, pair, near, far, basis, step, handed, whole):
+    width = back.shape[0]
+
+    @pl.when((ids[0] == 1) | (ids[0] == 2))
+    def _():
+        for c, block in enumerate((back, pair, near, far)):
+            whole[at_block(ids[c], width), :] = block[...]
+        handed[...] = dot(basis[at_block(ids[1], width), :], whole[...], 1, 0).astype(handed.dtype)
+        step[...] = dot(basis[at_block(ids[0], width), :], whole[...], 1, 0).astype(step.dtype)
+
+
+def update_both(ids, blocks, basis):
+    shape = jax.ShapeDtypeStruct(blocks[0].shape, blocks[0].dtype)
+    vmem = pl.BlockSpec(memory_space=pltpu.VMEM)
+    return pl.pallas_call(
+        update_kernel,
+        out_shape=[shape, shape],
+        in_specs=[pl.BlockSpec(memory_space=pltpu.SMEM)] + [vmem] * 5,
+        out_specs=[vmem, vmem],
+        scratch_shapes=[pltpu.VMEM(basis.shape, blocks[0].dtype)],
+        name="update_both",
+    )(ids, *blocks, basis)
+
+
 SWAP = [(0, 1), (1, 0), (2, 3), (3, 2)]
 MIDDLE = [(1, 2), (2, 1)]
 OVER = [(0, 2), (3, 1)]
@@ -92,8 +144,8 @@
 OUTWARD = [(1, 0), (2, 3)]
 
 
-def moments(turned, basis, factor, moment, second):
-    rotated = factor * dot(turned, basis, 1, 0)
+def moments(rotated, basis, factor, moment, second):
+    rotated = factor * rotated
     new_moment = beta_one * moment + (1.0 - beta_one) * rotated
     new_second = beta_two * second + (1.0 - beta_two) * rotated * rotated
     scaled = (new_moment / (jnp.sqrt(new_second) + epsilon)).astype(jnp.bfloat16)
@@ -116,23 +168,17 @@
     if line:
         near_at = jnp.where(upper, 1, 2)
         ids = [place, place ^ 1, near_at, jnp.where(upper, 0, 3)]
-    else:
-        ids = [lax.rem(place + k, size) for k in range(size)]
-
-    def rearranged(matrix):
-        matrix = jnp.concatenate([lax.dynamic_slice_in_dim(matrix, i * width, width, 0) for i in ids], axis=0)
-        return jnp.concatenate([lax.dynamic_slice_in_dim(matrix, i * width, width, 1) for i in ids], axis=1)
+        order_ids = jnp.stack(ids).astype(jnp.int32)
 
     turn = []
     for s in range(per):
-        turn.append(rearranged(basis_right[s]))
-
+        turn.append(lax.dynamic_slice_in_dim(basis_right[s], place * width, width, 1))
     own = []
     if line:
         sent, total = take(grad, owner_slots, owners)
         piece = lax.all_to_all(sent, "fsdp", split_axis=0, concat_axis=0, tiled=True)
         total = total_over(total, ("blk",))
-        piece, total, *turn = lax.optimization_barrier((piece, total, *turn))
+        piece, total, turn, order_ids = lax.optimization_barrier((piece, total, turn, order_ids))
         total = lax.all_to_all(total, "fsdp", split_axis=0, concat_axis=0, tiled=True)
         total = jnp.sum(total[:, 0])
         for s in range(per):
@@ -148,55 +194,41 @@
     grad_rms = jnp.sqrt(total / (blocks * order * order))
     factor = jnp.minimum(1.0, clip_level / grad_rms)
 
-    def canonical(parts):
+    own = own[:1] + [lax.optimization_barrier(block) for block in own[1:]]
+
+    gathered, rotations = [], []
+    for s in range(per):
         if line:
-            a, b, c, d = parts
-            low = jnp.where(place == 0, a, b), jnp.where(place == 0, b, a)
-            high = jnp.where(place == 2, a, b), jnp.where(place == 2, b, a)
-            return [
-                jnp.where(upper, d, low[0]),
-                jnp.where(upper, c, low[1]),
-                jnp.where(upper, high[0], c),
-                jnp.where(upper, high[1], d),
-            ]
-        return [sum(jnp.where(i == k, p, 0) for i, p in zip(ids, parts)) for k in range(len(parts))]
-
-    gathered = []
-    if line:
-        pairs = send(jnp.stack(own), SWAP)
-        for s in range(per):
-            pair = pairs[s]
             near = send(own[s], MIDDLE)
+            pair = send(own[s], SWAP)
             far = send(own[s], OVER)
-            passed = send(jnp.stack([near, far]), OUTWARD)
-            near, far = jnp.where(end, passed[0], near), jnp.where(end, passed[1], far)
-            gathered.append([own[s], pair, near, far])
-    else:
-        for s in range(per):
-            every = lax.all_gather(own[s], "blk")
-            gathered.append([lax.dynamic_index_in_dim(every, i, 0, keepdims=False) for i in ids])
+            passed_near = send(near, OUTWARD)
+            passed_far = send(far, OUTWARD)
+            blocks_now = [own[s], pair, near, far, passed_near, passed_far]
+            rotated, columns = turn_own(order_ids, blocks_now, turn[s], basis_left[s])
+        else:
+            columns = lax.all_gather(own[s], "blk", axis=0, tiled=True)
+            rotated = dot(dot(turn[s], columns, 0, 0).astype(jnp.bfloat16), basis_left[s], 1, 0)
+        gathered.append(columns)
+        rotations.append(rotated)
 
     lefts, rights, moms, secs = [], [], [], []
     placed = None if line else jnp.zeros_like(grad)
     for s in range(per):
-        columns = jnp.concatenate(gathered[s], axis=0)
-        turned = dot(turn[s][:, :width], columns, 0, 0).astype(jnp.bfloat16)
-        new_moment, new_second, back = moments(turned, basis_left[s], factor, moment[s].T, second[s].T)
+        new_moment, new_second, back = moments(rotations[s], basis_left[s], factor, moment[s].T, second[s].T)
         moms.append(new_moment.T)
         secs.append(new_second.T)
         if line:
             near = send(back, MIDDLE)
             far = send(back, OVER)
             pair = send(back, INWARD)
-            backs = jnp.concatenate([back, pair, near, far], axis=0)
-            outer_step = dot(backs, turn[s][width : 2 * width], 0, 1).astype(jnp.bfloat16)
-            handed = send(outer_step, OUTWARD)
-            step = dot(backs, turn[s][:width], 0, 1).astype(jnp.bfloat16)
-            step = jnp.where(end, handed, step)
+            step, handed = update_both(order_ids, [back, pair, near, far], basis_right[s])
+            handed = send(handed, OUTWARD)
+            step = jnp.where(end, handed, step).T
         else:
-            every = lax.all_gather(back, "blk")
-            backs = jnp.concatenate([lax.dynamic_index_in_dim(every, i, 0, keepdims=False) for i in ids], axis=0)
-            step = dot(backs, turn[s][:width], 0, 1).astype(jnp.bfloat16)
+            backs = lax.all_gather(back, "blk", axis=0, tiled=True)
+            right_rows = lax.dynamic_slice_in_dim(basis_right[s], place * width, width, 0)
+            step = dot(backs, right_rows, 0, 1).astype(jnp.bfloat16)
         step = step.reshape(owners, rows, width)
         returned = lax.all_to_all(step, "fsdp", split_axis=0, concat_axis=0, tiled=True)
         if line:
@@ -204,14 +236,17 @@
         else:
             placed = placed.at[slots[:, s]].set(returned, unique_indices=True, mode="promise_in_bounds")
 
+        columns = gathered[s]
         own_rows = lax.dynamic_slice_in_dim(columns, place * width, width, 1)
         outer_left = dot(own_rows, columns, 0, 0)
-        outer_right = jnp.concatenate(canonical([dot(own[s], g, 1, 1) for g in gathered[s]]), axis=1)
+        outer_right = dot(own[s], columns, 1, 1)
         weight = (1.0 - stat_decay) * (factor * factor)
         lefts.append((stat_decay * stat_left[s].T + weight * outer_left).T)
         rights.append((stat_decay * stat_right[s].T + weight * outer_right).T)
 
-    return (placed, jnp.stack(lefts), jnp.stack(rights), jnp.stack(moms), jnp.stack(secs), grad_rms)
+    stacked = [jnp.stack(parts) for parts in (lefts, rights)]
+    stacked += [jnp.stack(parts) for parts in (moms, secs)]
+    return (placed, *stacked, grad_rms)
 
 
 def solution(mesh):

time: 142 us -> 150 us (1.056)
  starting transfers between devices: 49.3 us -> 67.4 us
  matrix products: 24.8 us -> 8.31 us
  Pallas kernels: 4.88 us -> 17.3 us
  other arithmetic: 15.2 us -> 11.5 us
  waiting for transfers between devices: 33.9 us -> 30.3 us
    ppermute x15 -> x18, starting transfers between devices: 28.8 us -> 47.6 us  [send(): return lax.ppermute(value, 'blk', pairs)]
    dot_general x18 -> x6, matrix products: 24.8 us -> 8.31 us  [dot(): lax.dot_general(a, b, (((da,), (db,)), ((), ())), preferred_element_type=...]
    pallas_call x0 -> x4, Pallas kernels: none -> 12.3 us  [the longest x2 7.26 us: turn_own(): pl.pallas_call(turn_kernel, out_shape=[jax.ShapeDtypeStruct(blocks[0].sha...]
    ppermute x15 -> x18, waiting for transfers between devices: 17.6 us -> 12.9 us  [send(): return lax.ppermute(value, 'blk', pairs)]
    concatenate x6 -> x0, other arithmetic: 3.34 us -> none  [the longest x2 3.03 us: rearranged(): jnp.concatenate([lax.dynamic_slice_in_dim(matrix, i * width, width, 1) fo...]
    all_to_all x1, waiting for transfers between devices: 0.01 us -> 2.87 us  [whole_step(): lax.all_to_all(sent, 'fsdp', split_axis=0, concat_axis=0, tiled=True)]
    squeeze x1 -> x2, local copies, waits for them, and re-layouts: 0.74 us -> 3.26 us  [the longest x1 1.71 us: whole_step(): basis_right[s]]
    all_to_all x2, waiting for transfers between devices: 10.9 us -> 8.74 us  [whole_step(): lax.all_to_all(step, 'fsdp', split_axis=0, concat_axis=0, tiled=True)]
  transfers between devices with their start and end apart: 21 -> 24, of which waited for: 7 -> 8; matrix products, arithmetic and copies ran while one was open for 33% -> 18% of each run, Pallas kernels for 1% -> 9%
where the time goes in v2:
time: 150 us; the launch traced here: 149 us
  starting transfers between devices  67.4 us (45%)
  waiting for transfers between devices  30.3 us (20%)
  Pallas kernels  17.3 us (12%)
  other arithmetic  11.5 us (8%)
  local copies, waits for them, and re-layouts  10.8 us (7%)
  matrix products  8.31 us (6%)
  between operations  2.88 us (2%)
    ppermute x18, starting transfers between devices, send(): return lax.ppermute(value, 'blk', pairs)  47.6 us
    ppermute x18, waiting for transfers between devices, send(): return lax.ppermute(value, 'blk', pairs)  12.9 us
    all_to_all x2, waiting for transfers between devices, whole_step(): lax.all_to_all(step, 'fsdp', split_axis=0, concat_axis=0, tiled=True)  8.74 us
    dot_general x6, matrix products, dot(): lax.dot_general(a, b, (((da,), (db,)), ((), ())), preferred_element_type=...  8.31 us
    pallas_call x2, Pallas kernels, turn_own(): pl.pallas_call(turn_kernel, out_shape=[jax.ShapeDtypeStruct(blocks[0].sha...  7.26 us
    all_to_all x2, starting transfers between devices, whole_step(): lax.all_to_all(step, 'fsdp', split_axis=0, concat_axis=0, tiled=True)  6.91 us
    all_to_all x1, starting transfers between devices, whole_step(): lax.all_to_all(sent, 'fsdp', split_axis=0, concat_axis=0, tiled=True)  5.33 us
    pallas_call x2, Pallas kernels, update_both(): pl.pallas_call(update_kernel, out_shape=[shape, shape], in_specs=[pl.Bloc...  5.04 us
  transfers between devices with their start and end apart: 24, of which 8 were waited for; matrix products, arithmetic and copies ran while one was open for 18% of the time, Pallas kernels for 9%

profile of v2, /device:TPU:0, one launch (start us, length us, event | category | flops | bytes accessed | tf_op | source)
XLA Modules:
  0.0 148.5 jit_solution(4992180951957978597)
XLA Ops:
  0.6 2.3 %take.1 = (bf16[8,192,192]{2,1,0:T(8,128)(2,1)}, f32[8,128]{1,0:T(8,128)}) custom-call(s32[16]{0:T(128)} %slots.1, bf16[16,96,192]{2,1,0:T(8,128)(2,1)} %grad.1), custom_call_target="tpu_custom_call" | custom-call | tf_op jit(solution)/shard_map/take/pallas_call | solution.py:52
  3.0 5.3 %all-to-all-start = ((bf16[8,192,192]{2,1,0:T(8,128)(2,1)}), bf16[8,192,192]{2,1,0:T(8,128)(2,1)S(1)}, u32[]{:S(2)}, u32[]{:S(2)}) async-start(bf16[8,192,192]{2,1,0:T(8,128)(2,1)} %get-tuple-element.21), calls=%async_computation | async-start | bytes 1572864 | tf_op jit(solution)/shard_map/all_to_all | solution.py:179
  8.3 1.6 %collective-permute-start = (f32[8,128]{1,0:T(8,128)S(1)}, f32[8,128]{1,0:T(8,128)S(1)}, u32[]{:S(2)}, u32[]{:S(2)}) collective-permute-start(f32[8,128]{1,0:T(8,128)S(1)} %copy-done.17), channel_id=1, source_target_pairs={{0,1},{1,0},{2,3},{3,2},{4,5},{5,4},{6,7},{7,6},{8,9},{9,8},{10,11... | collective-permute-start | bytes 12296 | tf_op jit(solution)/shard_map/ppermute | solution.py:28
  10.0 1.7 %slice_bitcast_fusion.5 = (bf16[768,768]{1,0:T(8,128)(2,1)}, bf16[768,768]{1,0:T(8,128)(2,1)}, bf16[1,768,768]{2,1,0:T(8,128)(2,1)S(1)}, bf16[1,768,768]{2,1,0:T(8,128)(2,1)S(1)}) fusion(bf16[2,768,768]{2,1,0:T(8,128)(2,1)S(1)} %copy-done.4), kind=kLoop, calls=%fused_computation.57 | loop fusion | bytes 7077888 | tf_op jit(solution)/shard_map/squeeze | solution.py:175
  12.9 2.6 %collective-permute-start.1 = (f32[8,128]{1,0:T(8,128)S(1)}, f32[8,128]{1,0:T(8,128)S(1)}, u32[]{:S(2)}, u32[]{:S(2)}) collective-permute-start(f32[8,128]{1,0:T(8,128)S(1)} %add.46), channel_id=1, source_target_pairs={{0,2},{1,3},{2,0},{3,1},{4,6},{5,7},{6,4},{7,5},{8,10},{9,11},{10,... | collective-permute-start | bytes 12296 | tf_op jit(solution)/shard_map/ppermute | solution.py:28
  18.0 2.9 %all-to-all-done = bf16[8,192,192]{2,1,0:T(8,128)(2,1)S(1)} async-done(((bf16[8,192,192]{2,1,0:T(8,128)(2,1)}), bf16[8,192,192]{2,1,0:T(8,128)(2,1)S(1)}, u32[]{:S(2)}, u32[]{:S(2)}) %all-to-all-start) | async-done | bytes 589856 | tf_op jit(solution)/shard_map/all_to_all | solution.py:179
  22.9 1.4 collective-permute-start.3
  24.3 6.2 %collective-permute-start.4 = (bf16[192,768]{1,0:T(8,128)(2,1)S(1)}, bf16[192,768]{1,0:T(8,128)(2,1)}, u32[]{:S(2)}, u32[]{:S(2)}) collective-permute-start(bf16[192,768]{1,0:T(8,128)(2,1)S(1)} %bitcast.109), channel_id=1, source_target_pairs={{0,2},{3,1},{4,6},{7,5},{8,10},{11,9},{12,14},{15,13},{16,18},{19,... | collective-permute-start | bytes 884744 | tf_op jit(solution)/shard_map/ppermute | solution.py:34
  30.7 1.5 %collective-permute-start.12 = (bf16[192,768]{1,0:T(8,128)(2,1)S(1)}, bf16[192,768]{1,0:T(8,128)(2,1)}, u32[]{:S(2)}, u32[]{:S(2)}) collective-permute-start(bf16[192,768]{1,0:T(8,128)(2,1)S(1)} %bitcast.116), channel_id=1, source_target_pairs={{1,2},{2,1},{5,6},{6,5},{9,10},{10,9},{13,14},{14,13},{17,18},{18,... | collective-permute-start | bytes 884744 | tf_op jit(solution)/shard_map/ppermute | solution.py:34
  32.2 6.6 %collective-permute-start.13 = (bf16[192,768]{1,0:T(8,128)(2,1)S(1)}, bf16[192,768]{1,0:T(8,128)(2,1)}, u32[]{:S(2)}, u32[]{:S(2)}) collective-permute-start(bf16[192,768]{1,0:T(8,128)(2,1)S(1)} %bitcast.117), channel_id=1, source_target_pairs={{0,2},{3,1},{4,6},{7,5},{8,10},{11,9},{12,14},{15,13},{16,18},{19,... | collective-permute-start | bytes 884744 | tf_op jit(solution)/shard_map/ppermute | solution.py:34
  41.5 1.6 %slice_bitcast_fusion = (bf16[768,768]{1,0:T(8,128)(2,1)}, bf16[768,768]{1,0:T(8,128)(2,1)}) fusion(bf16[2,768,768]{2,1,0:T(8,128)(2,1)S(1)} %copy-done.5), kind=kLoop, calls=%fused_computation.18 | loop fusion | bytes 4718592 | tf_op jit(solution)/shard_map/squeeze | solution.py:208
  43.1 3.3 %all-to-all-start.1 = ((f32[8,1,128]{2,1,0:T(1,128)}), f32[8,1,128]{2,1,0:T(1,128)S(1)}, u32[]{:S(2)}, u32[]{:S(2)}) async-start(f32[8,1,128]{2,1,0:T(1,128)} %bitcast.9), calls=%async_computation.1 | async-start | bytes 8192 | tf_op jit(solution)/shard_map/all_to_all | solution.py:182
  46.6 4.4 %all-to-all-done.1 = f32[8,1,128]{2,1,0:T(1,128)S(1)} async-done(((f32[8,1,128]{2,1,0:T(1,128)}), f32[8,1,128]{2,1,0:T(1,128)S(1)}, u32[]{:S(2)}, u32[]{:S(2)}) %all-to-all-start.1) | async-done | bytes 4128 | tf_op jit(solution)/shard_map/all_to_all | solution.py:182
  52.4 8.0 %collective-permute-start.11 = (bf16[192,768]{1,0:T(8,128)(2,1)S(1)}, bf16[192,768]{1,0:T(8,128)(2,1)S(1)}, u32[]{:S(2)}, u32[]{:S(2)}) collective-permute-start(bf16[192,768]{1,0:T(8,128)(2,1)S(1)} %bitcast.118), channel_id=1, source_target_pairs={{0,1},{1,0},{2,3},{3,2},{4,5},{5,4},{6,7},{7,6},{8,9},{9,8},{10,11... | collective-permute-start | bytes 884744 | tf_op jit(solution)/shard_map/ppermute | solution.py:34
  63.0 3.6 %turn_own.2 = (f32[192,768]{1,0:T(8,128)}, bf16[768,768]{1,0:T(8,128)(2,1)}) custom-call(s32[4]{0:T(128)} %pad_add_fusion.ids, bf16[192,768]{1,0:T(8,128)(2,1)} %bitcast.111, bf16[192,768]{1,0:T(8,128)(2,1)} %collective-permute-done.2.pair, bf16[192,768]{1,0:T(8,128)(2,1)} %collective-permute-done.3.near, bf16[192,768]{1,0:T(8,128)(2,1)} %collective-permute-done.4.far, ...), custom_call_target="tpu_custom_call" | custom-call | tf_op jit(solution)/shard_map/turn_own/pallas_call | solution.py:104
  66.6 2.9 %convolution_convert_fusion.1.back = bf16[192,768]{1,0:T(8,128)(2,1)} fusion(f32[2,768,192]{1,2,0:T(8,128)} %param.14, f32[192,768]{1,0:T(8,128)} %get-tuple-element.27, f32[]{:T(128)S(6)} %min_shard_map.3, f32[2,768,192]{1,2,0:T(8,128)} %param.15, bf16[2,768,768]{2,1,0:T(8,128)(2,1)S(1)} %copy-done.5), kind=kOutput, calls=%fused_computation.13 | convolution fusion | flops 228261888 | bytes 3244036 | tf_op jit(solution)/shard_map/dot_general | solution.py:17
  69.5 6.7 %collective-permute-start.7 = (bf16[192,768]{1,0:T(8,128)(2,1)}, bf16[192,768]{1,0:T(8,128)(2,1)}, u32[]{:S(2)}, u32[]{:S(2)}) collective-permute-start(bf16[192,768]{1,0:T(8,128)(2,1)} %convolution_convert_fusion.1.back), channel_id=1, source_target_pairs={{0,1},{3,2},{4,5},{7,6},{8,9},{11,10},{12,13},{15,14},{16,17},{19,... | collective-permute-start | bytes 884744 | tf_op jit(solution)/shard_map/ppermute | solution.py:34
  77.6 2.4 %collective-permute-done.15.passed_far = bf16[192,768]{1,0:T(8,128)(2,1)} collective-permute-done((bf16[192,768]{1,0:T(8,128)(2,1)}, bf16[192,768]{1,0:T(8,128)(2,1)}, u32[]{:S(2)}, u32[]{:S(2)}) %collective-permute-start.15) | collective-permute-done | bytes 294944 | tf_op jit(solution)/shard_map/ppermute | solution.py:34
  80.0 3.6 %turn_own.3 = (f32[192,768]{1,0:T(8,128)}, bf16[768,768]{1,0:T(8,128)(2,1)}) custom-call(s32[4]{0:T(128)} %pad_add_fusion.ids, bf16[192,768]{1,0:T(8,128)(2,1)} %bitcast.119, bf16[192,768]{1,0:T(8,128)(2,1)} %copy-done.16, bf16[192,768]{1,0:T(8,128)(2,1)} %collective-permute-done.12.near, bf16[192,768]{1,0:T(8,128)(2,1)} %collective-permute-done.13.far, ...), custom_call_target="tpu_custom_call" | custom-call | tf_op jit(solution)/shard_map/turn_own/pallas_call | solution.py:104
  83.6 2.3 %convolution_convert_fusion.back = bf16[192,768]{1,0:T(8,128)(2,1)S(1)} fusion(f32[2,768,192]{1,2,0:T(8,128)} %param.14, f32[192,768]{1,0:T(8,128)} %get-tuple-element.31, f32[]{:T(128)S(6)} %min_shard_map.3, f32[2,768,192]{1,2,0:T(8,128)} %param.15, bf16[2,768,768]{2,1,0:T(8,128)(2,1)S(1)} %copy-done.5), kind=kOutput, calls=%fused_computation.12 | convolution fusion | flops 228261888 | bytes 3244036 | tf_op jit(solution)/shard_map/dot_general | solution.py:17
  85.9 1.5 collective-permute-start.16
  88.1 4.0 %collective-permute-start.18 = (bf16[192,768]{1,0:T(8,128)(2,1)S(1)}, bf16[192,768]{1,0:T(8,128)(2,1)S(1)}, u32[]{:S(2)}, u32[]{:S(2)}) collective-permute-start(bf16[192,768]{1,0:T(8,128)(2,1)S(1)} %convolution_convert_fusion.back), channel_id=1, source_target_pairs={{0,2},{3,1},{4,6},{7,5},{8,10},{11,9},{12,14},{15,13},{16,18},{19,... | collective-permute-start | bytes 884744 | tf_op jit(solution)/shard_map/ppermute | solution.py:34
  97.7 2.0 %collective-permute-start.9 = (bf16[192,768]{1,0:T(8,128)(2,1)}, bf16[192,768]{1,0:T(8,128)(2,1)}, u32[]{:S(2)}, u32[]{:S(2)}) collective-permute-start(bf16[192,768]{1,0:T(8,128)(2,1)} %convolution_convert_fusion.1.back), channel_id=1, source_target_pairs={{0,2},{3,1},{4,6},{7,5},{8,10},{11,9},{12,14},{15,13},{16,18},{19,... | collective-permute-start | bytes 884744 | tf_op jit(solution)/shard_map/ppermute | solution.py:34
  101.3 2.5 %update_both.3 = (bf16[192,768]{1,0:T(8,128)(2,1)}, bf16[192,768]{1,0:T(8,128)(2,1)}) custom-call(s32[4]{0:T(128)} %pad_add_fusion.ids, bf16[192,768]{1,0:T(8,128)(2,1)} %copy-done.10, bf16[192,768]{1,0:T(8,128)(2,1)} %copy-done.11, bf16[192,768]{1,0:T(8,128)(2,1)} %copy-done.12, bf16[192,768]{1,0:T(8,128)(2,1)} %copy-done.13, ...), custom_call_target="tpu_custom_call" | custom-call | tf_op jit(solution)/shard_map/update_both/pallas_call | solution.py:130
  105.1 2.2 %fusion.15 = (f32[1,768,192]{1,2,0:T(8,128)S(1)}, f32[1,768,192]{1,2,0:T(8,128)S(1)}, f32[1,768,192]{1,2,0:T(8,128)S(1)}, f32[1,768,192]{1,2,0:T(8,128)S(1)}) fusion(f32[192,768]{1,0:T(8,128)} %get-tuple-element.31, f32[]{:T(128)S(6)} %min_shard_map.3, f32[2,768,192]{1,2,0:T(8,128)} %param.14, f32[192,768]{1,0:T(8,128)S(1)} %copy-done.9, ...), kind=kLoop, calls=%fused_computation.37 | loop fusion | flops 2359296 | bytes 5898244 | tf_op jit(solution)/shard_map/stack | solution.py:248
  107.3 2.5 %update_both.2 = (bf16[192,768]{1,0:T(8,128)(2,1)}, bf16[192,768]{1,0:T(8,128)(2,1)}) custom-call(s32[4]{0:T(128)} %pad_add_fusion.ids, bf16[192,768]{1,0:T(8,128)(2,1)} %convolution_convert_fusion.1.back, bf16[192,768]{1,0:T(8,128)(2,1)} %collective-permute-done.7.pair, bf16[192,768]{1,0:T(8,128)(2,1)} %collective-permute-done.8.near, ...), custom_call_target="tpu_custom_call" | custom-call | tf_op jit(solution)/shard_map/update_both/pallas_call | solution.py:130
  111.1 9.6 %collective-permute-done.19 = bf16[192,768]{1,0:T(8,128)(2,1)} collective-permute-done((bf16[192,768]{1,0:T(8,128)(2,1)}, bf16[192,768]{1,0:T(8,128)(2,1)}, u32[]{:S(2)}, u32[]{:S(2)}) %collective-permute-start.19) | collective-permute-done | bytes 294944 | tf_op jit(solution)/shard_map/ppermute | solution.py:34
  122.6 3.5 %all-to-all-start.3 = ((bf16[8,96,192]{2,1,0:T(8,128)(2,1)}), bf16[8,96,192]{2,1,0:T(8,128)(2,1)S(1)}, u32[]{:S(2)}, u32[]{:S(2)}) async-start(bf16[8,96,192]{2,1,0:T(8,128)(2,1)} %bitcast.114), calls=%async_computation.3 | async-start | bytes 786432 | tf_op jit(solution)/shard_map/all_to_all | solution.py:233
  126.1 2.3 %pad_maximum_fusion.1 = f32[2,768,192]{1,2,0:T(8,128)} fusion(f32[1,768,192]{1,2,0:T(8,128)} %fusion.7, f32[1,768,192]{1,2,0:T(8,128)S(1)} %fusion.5), kind=kLoop, calls=%fused_computation.15 | loop fusion | flops 294912 | bytes 2359296 | tf_op jit(solution)/shard_map/stack | solution.py:247
  130.3 4.0 %all-to-all-done.3.returned = bf16[8,96,192]{2,1,0:T(8,128)(2,1)S(1)} async-done(((bf16[8,96,192]{2,1,0:T(8,128)(2,1)}), bf16[8,96,192]{2,1,0:T(8,128)(2,1)S(1)}, u32[]{:S(2)}, u32[]{:S(2)}) %all-to-all-start.3) | async-done | bytes 294944 | tf_op jit(solution)/shard_map/all_to_all | solution.py:233
  134.3 3.5 %all-to-all-start.2 = ((bf16[8,96,192]{2,1,0:T(8,128)(2,1)}), bf16[8,96,192]{2,1,0:T(8,128)(2,1)S(1)}, u32[]{:S(2)}, u32[]{:S(2)}) async-start(bf16[8,96,192]{2,1,0:T(8,128)(2,1)} %bitcast.113), calls=%async_computation.2 | async-start | bytes 786432 | tf_op jit(solution)/shard_map/all_to_all | solution.py:233
  141.3 4.7 %all-to-all-done.2.returned = bf16[8,96,192]{2,1,0:T(8,128)(2,1)S(1)} async-done(((bf16[8,96,192]{2,1,0:T(8,128)(2,1)}), bf16[8,96,192]{2,1,0:T(8,128)(2,1)S(1)}, u32[]{:S(2)}, u32[]{:S(2)}) %all-to-all-start.2) | async-done | bytes 294944 | tf_op jit(solution)/shard_map/all_to_all | solution.py:233
  (88 shorter events, 32.5 us)
Async XLA Ops:
  0.6 9.3 %copy-start.4 = (bf16[2,768,768]{2,1,0:T(8,128)(2,1)S(1)}, bf16[2,768,768]{2,1,0:T(8,128)(2,1)}, u32[]{:S(2)}) copy-start(bf16[2,768,768]{2,1,0:T(8,128)(2,1)} %param.13) | copy-start | bytes 7077892
  3.0 17.9 %all-to-all-start = ((bf16[8,192,192]{2,1,0:T(8,128)(2,1)}), bf16[8,192,192]{2,1,0:T(8,128)(2,1)S(1)}, u32[]{:S(2)}, u32[]{:S(2)}) async-start(bf16[8,192,192]{2,1,0:T(8,128)(2,1)} %get-tuple-element.21), calls=%async_computation | async-start | bytes 1572864 | tf_op jit(solution)/shard_map/all_to_all | solution.py:179
  8.3 4.6 %collective-permute-start = (f32[8,128]{1,0:T(8,128)S(1)}, f32[8,128]{1,0:T(8,128)S(1)}, u32[]{:S(2)}, u32[]{:S(2)}) collective-permute-start(f32[8,128]{1,0:T(8,128)S(1)} %copy-done.17), channel_id=1, source_target_pairs={{0,1},{1,0},{2,3},{3,2},{4,5},{5,4},{6,7},{7,6},{8,9},{9,8},{10,11... | collective-permute-start | bytes 12296 | tf_op jit(solution)/shard_map/ppermute | solution.py:28
  12.9 4.5 %collective-permute-start.1 = (f32[8,128]{1,0:T(8,128)S(1)}, f32[8,128]{1,0:T(8,128)S(1)}, u32[]{:S(2)}, u32[]{:S(2)}) collective-permute-start(f32[8,128]{1,0:T(8,128)S(1)} %add.46), channel_id=1, source_target_pairs={{0,2},{1,3},{2,0},{3,1},{4,6},{5,7},{6,4},{7,5},{8,10},{9,11},{10,... | collective-permute-start | bytes 12296 | tf_op jit(solution)/shard_map/ppermute | solution.py:28
  20.9 20.6 %copy-start.5 = (bf16[2,768,768]{2,1,0:T(8,128)(2,1)S(1)}, bf16[2,768,768]{2,1,0:T(8,128)(2,1)}, u32[]{:S(2)}) copy-start(bf16[2,768,768]{2,1,0:T(8,128)(2,1)} %param.12) | copy-start | bytes 7077892
  22.9 20.1 %copy-start.2 = (bf16[768,192]{0,1:T(8,128)(2,1)}, bf16[768,192]{0,1:T(8,128)(2,1)S(1)}, u32[]{:S(2)}) copy-start(bf16[768,192]{0,1:T(8,128)(2,1)S(1)} %copy.28) | copy-start | bytes 884740
  22.9 15.9 %collective-permute-start.3 = (bf16[192,768]{1,0:T(8,128)(2,1)S(1)}, bf16[192,768]{1,0:T(8,128)(2,1)}, u32[]{:S(2)}, u32[]{:S(2)}) collective-permute-start(bf16[192,768]{1,0:T(8,128)(2,1)S(1)} %bitcast.108), channel_id=1, source_target_pairs={{1,2},{2,1},{5,6},{6,5},{9,10},{10,9},{13,14},{14,13},{17,18},{18,... | collective-permute-start | bytes 884744 | tf_op jit(solution)/shard_map/ppermute | solution.py:34
  24.3 15.8 %collective-permute-start.4 = (bf16[192,768]{1,0:T(8,128)(2,1)S(1)}, bf16[192,768]{1,0:T(8,128)(2,1)}, u32[]{:S(2)}, u32[]{:S(2)}) collective-permute-start(bf16[192,768]{1,0:T(8,128)(2,1)S(1)} %bitcast.109), channel_id=1, source_target_pairs={{0,2},{3,1},{4,6},{7,5},{8,10},{11,9},{12,14},{15,13},{16,18},{19,... | collective-permute-start | bytes 884744 | tf_op jit(solution)/shard_map/ppermute | solution.py:34
  30.5 21.9 %collective-permute-start.2 = (bf16[192,768]{1,0:T(8,128)(2,1)S(1)}, bf16[192,768]{1,0:T(8,128)(2,1)}, u32[]{:S(2)}, u32[]{:S(2)}) collective-permute-start(bf16[192,768]{1,0:T(8,128)(2,1)S(1)} %bitcast.110), channel_id=1, source_target_pairs={{0,1},{1,0},{2,3},{3,2},{4,5},{5,4},{6,7},{7,6},{8,9},{9,8},{10,11... | collective-permute-start | bytes 884744 | tf_op jit(solution)/shard_map/ppermute | solution.py:34
  30.7 21.7 %copy-start.8 = (bf16[768,192]{0,1:T(8,128)(2,1)}, bf16[768,192]{0,1:T(8,128)(2,1)S(1)}, u32[]{:S(2)}) copy-start(bf16[768,192]{0,1:T(8,128)(2,1)S(1)} %copy.29) | copy-start | bytes 884740
  30.7 12.3 %copy-start.18 = (s32[16]{0:T(128)S(1)}, s32[16]{0:T(128)}, u32[]{:S(2)}) copy-start(s32[16]{0:T(128)} %slots.1) | copy-start | bytes 196
  30.7 29.7 %collective-permute-start.12 = (bf16[192,768]{1,0:T(8,128)(2,1)S(1)}, bf16[192,768]{1,0:T(8,128)(2,1)}, u32[]{:S(2)}, u32[]{:S(2)}) collective-permute-start(bf16[192,768]{1,0:T(8,128)(2,1)S(1)} %bitcast.116), channel_id=1, source_target_pairs={{1,2},{2,1},{5,6},{6,5},{9,10},{10,9},{13,14},{14,13},{17,18},{18,... | collective-permute-start | bytes 884744 | tf_op jit(solution)/shard_map/ppermute | solution.py:34
  32.2 29.5 %collective-permute-start.13 = (bf16[192,768]{1,0:T(8,128)(2,1)S(1)}, bf16[192,768]{1,0:T(8,128)(2,1)}, u32[]{:S(2)}, u32[]{:S(2)}) collective-permute-start(bf16[192,768]{1,0:T(8,128)(2,1)S(1)} %bitcast.117), channel_id=1, source_target_pairs={{0,2},{3,1},{4,6},{7,5},{8,10},{11,9},{12,14},{15,13},{16,18},{19,... | collective-permute-start | bytes 884744 | tf_op jit(solution)/shard_map/ppermute | solution.py:34
  38.8 24.2 %collective-permute-start.5 = (bf16[192,768]{1,0:T(8,128)(2,1)}, bf16[192,768]{1,0:T(8,128)(2,1)}, u32[]{:S(2)}, u32[]{:S(2)}) collective-permute-start(bf16[192,768]{1,0:T(8,128)(2,1)} %collective-permute-done.3.near), channel_id=1, source_target_pairs={{1,0},{2,3},{5,4},{6,7},{9,8},{10,11},{13,12},{14,15},{17,16},{18,... | collective-permute-start | bytes 884744 | tf_op jit(solution)/shard_map/ppermute | solution.py:34
  40.1 22.9 %collective-permute-start.6 = (bf16[192,768]{1,0:T(8,128)(2,1)}, bf16[192,768]{1,0:T(8,128)(2,1)}, u32[]{:S(2)}, u32[]{:S(2)}) collective-permute-start(bf16[192,768]{1,0:T(8,128)(2,1)} %collective-permute-done.4.far), channel_id=1, source_target_pairs={{1,0},{2,3},{5,4},{6,7},{9,8},{10,11},{13,12},{14,15},{17,16},{18,... | collective-permute-start | bytes 884744 | tf_op jit(solution)/shard_map/ppermute | solution.py:34
  43.1 8.0 %all-to-all-start.1 = ((f32[8,1,128]{2,1,0:T(1,128)}), f32[8,1,128]{2,1,0:T(1,128)S(1)}, u32[]{:S(2)}, u32[]{:S(2)}) async-start(f32[8,1,128]{2,1,0:T(1,128)} %bitcast.9), calls=%async_computation.1 | async-start | bytes 8192 | tf_op jit(solution)/shard_map/all_to_all | solution.py:182
  52.4 25.2 %collective-permute-start.11 = (bf16[192,768]{1,0:T(8,128)(2,1)S(1)}, bf16[192,768]{1,0:T(8,128)(2,1)S(1)}, u32[]{:S(2)}, u32[]{:S(2)}) collective-permute-start(bf16[192,768]{1,0:T(8,128)(2,1)S(1)} %bitcast.118), channel_id=1, source_target_pairs={{0,1},{1,0},{2,3},{3,2},{4,5},{5,4},{6,7},{7,6},{8,9},{9,8},{10,11... | collective-permute-start | bytes 884744 | tf_op jit(solution)/shard_map/ppermute | solution.py:34
  60.4 17.2 %collective-permute-start.14 = (bf16[192,768]{1,0:T(8,128)(2,1)}, bf16[192,768]{1,0:T(8,128)(2,1)}, u32[]{:S(2)}, u32[]{:S(2)}) collective-permute-start(bf16[192,768]{1,0:T(8,128)(2,1)} %collective-permute-done.12.near), channel_id=1, source_target_pairs={{1,0},{2,3},{5,4},{6,7},{9,8},{10,11},{13,12},{14,15},{17,16},{18,... | collective-permute-start | bytes 884744 | tf_op jit(solution)/shard_map/ppermute | solution.py:34
  61.7 18.3 %collective-permute-start.15 = (bf16[192,768]{1,0:T(8,128)(2,1)}, bf16[192,768]{1,0:T(8,128)(2,1)}, u32[]{:S(2)}, u32[]{:S(2)}) collective-permute-start(bf16[192,768]{1,0:T(8,128)(2,1)} %collective-permute-done.13.far), channel_id=1, source_target_pairs={{1,0},{2,3},{5,4},{6,7},{9,8},{10,11},{13,12},{14,15},{17,16},{18,... | collective-permute-start | bytes 884744 | tf_op jit(solution)/shard_map/ppermute | solution.py:34
  69.5 37.8 %collective-permute-start.7 = (bf16[192,768]{1,0:T(8,128)(2,1)}, bf16[192,768]{1,0:T(8,128)(2,1)}, u32[]{:S(2)}, u32[]{:S(2)}) collective-permute-start(bf16[192,768]{1,0:T(8,128)(2,1)} %convolution_convert_fusion.1.back), channel_id=1, source_target_pairs={{0,1},{3,2},{4,5},{7,6},{8,9},{11,10},{12,13},{15,14},{16,17},{19,... | collective-permute-start | bytes 884744 | tf_op jit(solution)/shard_map/ppermute | solution.py:34
  76.2 31.1 %collective-permute-start.8 = (bf16[192,768]{1,0:T(8,128)(2,1)}, bf16[192,768]{1,0:T(8,128)(2,1)}, u32[]{:S(2)}, u32[]{:S(2)}) collective-permute-start(bf16[192,768]{1,0:T(8,128)(2,1)} %convolution_convert_fusion.1.back), channel_id=1, source_target_pairs={{1,2},{2,1},{5,6},{6,5},{9,10},{10,9},{13,14},{14,13},{17,18},{18,... | collective-permute-start | bytes 884744 | tf_op jit(solution)/shard_map/ppermute | solution.py:34
  83.6 8.5 %copy-start = (bf16[768,768]{1,0:T(8,128)(2,1)S(1)}, bf16[768,768]{1,0:T(8,128)(2,1)}, u32[]{:S(2)}) copy-start(bf16[768,768]{1,0:T(8,128)(2,1)} %get-tuple-element.35) | copy-start | bytes 3538948
  83.6 8.5 %copy-start.6 = (f32[2,768,192]{1,2,0:T(8,128)S(1)}, f32[2,768,192]{1,2,0:T(8,128)}, u32[]{:S(2)}) copy-start(f32[2,768,192]{1,2,0:T(8,128)} %param.10) | copy-start | bytes 3538948
  85.9 11.8 %collective-permute-start.16 = (bf16[192,768]{1,0:T(8,128)(2,1)S(1)}, bf16[192,768]{1,0:T(8,128)(2,1)S(1)}, u32[]{:S(2)}, u32[]{:S(2)}) collective-permute-start(bf16[192,768]{1,0:T(8,128)(2,1)S(1)} %convolution_convert_fusion.back), channel_id=1, source_target_pairs={{0,1},{3,2},{4,5},{7,6},{8,9},{11,10},{12,13},{15,14},{16,17},{19,... | collective-permute-start | bytes 884744 | tf_op jit(solution)/shard_map/ppermute | solution.py:34
  87.4 12.3 %collective-permute-start.17 = (bf16[192,768]{1,0:T(8,128)(2,1)S(1)}, bf16[192,768]{1,0:T(8,128)(2,1)S(1)}, u32[]{:S(2)}, u32[]{:S(2)}) collective-permute-start(bf16[192,768]{1,0:T(8,128)(2,1)S(1)} %convolution_convert_fusion.back), channel_id=1, source_target_pairs={{1,2},{2,1},{5,6},{6,5},{9,10},{10,9},{13,14},{14,13},{17,18},{18,... | collective-permute-start | bytes 884744 | tf_op jit(solution)/shard_map/ppermute | solution.py:34
  88.1 12.5 %collective-permute-start.18 = (bf16[192,768]{1,0:T(8,128)(2,1)S(1)}, bf16[192,768]{1,0:T(8,128)(2,1)S(1)}, u32[]{:S(2)}, u32[]{:S(2)}) collective-permute-start(bf16[192,768]{1,0:T(8,128)(2,1)S(1)} %convolution_convert_fusion.back), channel_id=1, source_target_pairs={{0,2},{3,1},{4,6},{7,5},{8,10},{11,9},{12,14},{15,13},{16,18},{19,... | collective-permute-start | bytes 884744 | tf_op jit(solution)/shard_map/ppermute | solution.py:34
  97.7 9.6 %collective-permute-start.9 = (bf16[192,768]{1,0:T(8,128)(2,1)}, bf16[192,768]{1,0:T(8,128)(2,1)}, u32[]{:S(2)}, u32[]{:S(2)}) collective-permute-start(bf16[192,768]{1,0:T(8,128)(2,1)} %convolution_convert_fusion.1.back), channel_id=1, source_target_pairs={{0,2},{3,1},{4,6},{7,5},{8,10},{11,9},{12,14},{15,13},{16,18},{19,... | collective-permute-start | bytes 884744 | tf_op jit(solution)/shard_map/ppermute | solution.py:34
  103.8 16.9 %collective-permute-start.19 = (bf16[192,768]{1,0:T(8,128)(2,1)}, bf16[192,768]{1,0:T(8,128)(2,1)}, u32[]{:S(2)}, u32[]{:S(2)}) collective-permute-start(bf16[192,768]{1,0:T(8,128)(2,1)} %get-tuple-element.32), channel_id=1, source_target_pairs={{1,0},{2,3},{5,4},{6,7},{9,8},{10,11},{13,12},{14,15},{17,16},{18,... | collective-permute-start | bytes 884744 | tf_op jit(solution)/shard_map/ppermute | solution.py:34
  107.3 13.4 %copy-start.14 = (bf16[192,768]{1,0:T(8,128)(2,1)S(1)}, bf16[192,768]{1,0:T(8,128)(2,1)}, u32[]{:S(2)}) copy-start(bf16[192,768]{1,0:T(8,128)(2,1)} %get-tuple-element.33) | copy-start | bytes 884740
  109.8 18.6 %collective-permute-start.10 = (bf16[192,768]{1,0:T(8,128)(2,1)}, bf16[192,768]{1,0:T(8,128)(2,1)}, u32[]{:S(2)}, u32[]{:S(2)}) collective-permute-start(bf16[192,768]{1,0:T(8,128)(2,1)} %get-tuple-element.28), channel_id=1, source_target_pairs={{1,0},{2,3},{5,4},{6,7},{9,8},{10,11},{13,12},{14,15},{17,16},{18,... | collective-permute-start | bytes 884744 | tf_op jit(solution)/shard_map/ppermute | solution.py:34
  122.6 11.7 %all-to-all-start.3 = ((bf16[8,96,192]{2,1,0:T(8,128)(2,1)}), bf16[8,96,192]{2,1,0:T(8,128)(2,1)S(1)}, u32[]{:S(2)}, u32[]{:S(2)}) async-start(bf16[8,96,192]{2,1,0:T(8,128)(2,1)} %bitcast.114), calls=%async_computation.3 | async-start | bytes 786432 | tf_op jit(solution)/shard_map/all_to_all | solution.py:233
  134.3 11.7 %all-to-all-start.2 = ((bf16[8,96,192]{2,1,0:T(8,128)(2,1)}), bf16[8,96,192]{2,1,0:T(8,128)(2,1)S(1)}, u32[]{:S(2)}, u32[]{:S(2)}) async-start(bf16[8,96,192]{2,1,0:T(8,128)(2,1)} %bitcast.113), calls=%async_computation.2 | async-start | bytes 786432 | tf_op jit(solution)/shard_map/all_to_all | solution.py:233
  (11 other events, 28.8 us)

commit v3 on v2

--- a/solution.py
+++ b/solution.py
@@ -1,3 +1,5 @@
+import functools
+
 import jax
 import jax.numpy as jnp
 from jax import lax
@@ -113,7 +115,29 @@
     )(ids, *blocks, columns, basis)
 
 
-def update_kernel(ids, back, pair, near, far, basis, step, handed, whole):
+def update_kernel(which, ids, back, pair, near, far, basis, step, whole):
+    width = back.shape[0]
+
+    @pl.when((ids[0] == 1) | (ids[0] == 2))
+    def _():
+        for c, block in enumerate((back, pair, near, far)):
+            whole[at_block(ids[c], width), :] = block[...]
+        step[...] = dot(basis[at_block(ids[which], width), :], whole[...], 1, 0).astype(step.dtype)
+
+
+def update(which, ids, blocks, basis):
+    vmem = pl.BlockSpec(memory_space=pltpu.VMEM)
+    return pl.pallas_call(
+        functools.partial(update_kernel, which),
+        out_shape=jax.ShapeDtypeStruct(blocks[0].shape, blocks[0].dtype),
+        in_specs=[pl.BlockSpec(memory_space=pltpu.SMEM)] + [vmem] * 5,
+        out_specs=vmem,
+        scratch_shapes=[pltpu.VMEM(basis.shape, blocks[0].dtype)],
+        name="update_pair" if which else "update_own",
+    )(ids, *blocks, basis)
+
+
+def both_kernel(ids, back, pair, near, far, basis, step, handed, whole):
     width = back.shape[0]
 
     @pl.when((ids[0] == 1) | (ids[0] == 2))
@@ -128,7 +152,7 @@
     shape = jax.ShapeDtypeStruct(blocks[0].shape, blocks[0].dtype)
     vmem = pl.BlockSpec(memory_space=pltpu.VMEM)
     return pl.pallas_call(
-        update_kernel,
+        both_kernel,
         out_shape=[shape, shape],
         in_specs=[pl.BlockSpec(memory_space=pltpu.SMEM)] + [vmem] * 5,
         out_specs=[vmem, vmem],
@@ -222,7 +246,12 @@
             near = send(back, MIDDLE)
             far = send(back, OVER)
             pair = send(back, INWARD)
-            step, handed = update_both(order_ids, [back, pair, near, far], basis_right[s])
+            if s + 1 < per:
+                step, handed = update_both(order_ids, [back, pair, near, far], basis_right[s])
+            else:
+                handed = update(1, order_ids, [back, pair, near, far], basis_right[s])
+            if s + 1 == per:
+                step = update(0, order_ids, [back, pair, near, far], basis_right[s])
             handed = send(handed, OUTWARD)
             step = jnp.where(end, handed, step).T
         else:

time: 150 us -> 150 us (level)
  Pallas kernels: 17.3 us -> 19.5 us
    all_to_all x2, waiting for transfers between devices: 8.74 us -> 6.5 us  [whole_step(): lax.all_to_all(step, 'fsdp', split_axis=0, concat_axis=0, tiled=True)]
    pallas_call x2 -> x3, Pallas kernels: 5.04 us -> 7.25 us  [the longest x2 4.75 us: update(): pl.pallas_call(functools.partial(update_kernel, which), out_shape=jax.Sha...]
  transfers between devices with their start and end apart: 24 -> 24, of which waited for: 8 -> 8; matrix products, arithmetic and copies ran while one was open for 18% -> 17% of each run, Pallas kernels for 9% -> 11%
where the time goes in v3:
time: 150 us; the launch traced here: 149 us
  starting transfers between devices  66.7 us (44%)
  waiting for transfers between devices  28.9 us (19%)
  Pallas kernels  19.5 us (13%)
  other arithmetic  11.6 us (8%)
  local copies, waits for them, and re-layouts  11.5 us (8%)
  matrix products  7.6 us (5%)
  between operations  2.91 us (2%)
    ppermute x18, starting transfers between devices, send(): return lax.ppermute(value, 'blk', pairs)  46.9 us
    ppermute x18, waiting for transfers between devices, send(): return lax.ppermute(value, 'blk', pairs)  13.8 us
    dot_general x6, matrix products, dot(): lax.dot_general(a, b, (((da,), (db,)), ((), ())), preferred_element_type=...  7.6 us
    pallas_call x2, Pallas kernels, turn_own(): pl.pallas_call(turn_kernel, out_shape=[jax.ShapeDtypeStruct(blocks[0].sha...  7.24 us
    all_to_all x2, starting transfers between devices, whole_step(): lax.all_to_all(step, 'fsdp', split_axis=0, concat_axis=0, tiled=True)  6.91 us
    all_to_all x2, waiting for transfers between devices, whole_step(): lax.all_to_all(step, 'fsdp', split_axis=0, concat_axis=0, tiled=True)  6.5 us
    all_to_all x1, starting transfers between devices, whole_step(): lax.all_to_all(sent, 'fsdp', split_axis=0, concat_axis=0, tiled=True)  5.33 us
    pallas_call x2, Pallas kernels, update(): pl.pallas_call(functools.partial(update_kernel, which), out_shape=jax.Sha...  4.75 us
  transfers between devices with their start and end apart: 24, of which 8 were waited for; matrix products, arithmetic and copies ran while one was open for 17% of the time, Pallas kernels for 11%

profile of v3, /device:TPU:0, one launch (start us, length us, event | category | flops | bytes accessed | tf_op | source)
XLA Modules:
  0.0 148.7 jit_solution(1329026339480556383)
XLA Ops:
  0.6 2.3 %take.1 = (bf16[8,192,192]{2,1,0:T(8,128)(2,1)}, f32[8,128]{1,0:T(8,128)}) custom-call(s32[16]{0:T(128)} %slots.1, bf16[16,96,192]{2,1,0:T(8,128)(2,1)} %grad.1), custom_call_target="tpu_custom_call" | custom-call | tf_op jit(solution)/shard_map/take/pallas_call | solution.py:54
  3.0 5.3 %all-to-all-start = ((bf16[8,192,192]{2,1,0:T(8,128)(2,1)}), bf16[8,192,192]{2,1,0:T(8,128)(2,1)S(1)}, u32[]{:S(2)}, u32[]{:S(2)}) async-start(bf16[8,192,192]{2,1,0:T(8,128)(2,1)} %get-tuple-element.19), calls=%async_computation | async-start | bytes 1572864 | tf_op jit(solution)/shard_map/all_to_all | solution.py:203
  8.3 1.6 %collective-permute-start = (f32[8,128]{1,0:T(8,128)S(1)}, f32[8,128]{1,0:T(8,128)S(1)}, u32[]{:S(2)}, u32[]{:S(2)}) collective-permute-start(f32[8,128]{1,0:T(8,128)S(1)} %copy-done.15), channel_id=1, source_target_pairs={{0,1},{1,0},{2,3},{3,2},{4,5},{5,4},{6,7},{7,6},{8,9},{9,8},{10,11... | collective-permute-start | bytes 12296 | tf_op jit(solution)/shard_map/ppermute | solution.py:30
  10.0 1.7 %slice_bitcast_fusion.5 = (bf16[768,768]{1,0:T(8,128)(2,1)}, bf16[768,768]{1,0:T(8,128)(2,1)}, bf16[1,768,768]{2,1,0:T(8,128)(2,1)S(1)}, bf16[1,768,768]{2,1,0:T(8,128)(2,1)S(1)}) fusion(bf16[2,768,768]{2,1,0:T(8,128)(2,1)S(1)} %copy-done.4), kind=kLoop, calls=%fused_computation.57 | loop fusion | bytes 7077888 | tf_op jit(solution)/shard_map/squeeze | solution.py:199
  12.9 2.6 %collective-permute-start.1 = (f32[8,128]{1,0:T(8,128)S(1)}, f32[8,128]{1,0:T(8,128)S(1)}, u32[]{:S(2)}, u32[]{:S(2)}) collective-permute-start(f32[8,128]{1,0:T(8,128)S(1)} %add.46), channel_id=1, source_target_pairs={{0,2},{1,3},{2,0},{3,1},{4,6},{5,7},{6,4},{7,5},{8,10},{9,11},{10,... | collective-permute-start | bytes 12296 | tf_op jit(solution)/shard_map/ppermute | solution.py:30
  18.0 2.9 %all-to-all-done = bf16[8,192,192]{2,1,0:T(8,128)(2,1)S(1)} async-done(((bf16[8,192,192]{2,1,0:T(8,128)(2,1)}), bf16[8,192,192]{2,1,0:T(8,128)(2,1)S(1)}, u32[]{:S(2)}, u32[]{:S(2)}) %all-to-all-start) | async-done | bytes 589856 | tf_op jit(solution)/shard_map/all_to_all | solution.py:203
  24.3 6.2 %collective-permute-start.4 = (bf16[192,768]{1,0:T(8,128)(2,1)S(1)}, bf16[192,768]{1,0:T(8,128)(2,1)}, u32[]{:S(2)}, u32[]{:S(2)}) collective-permute-start(bf16[192,768]{1,0:T(8,128)(2,1)S(1)} %bitcast.109), channel_id=1, source_target_pairs={{0,2},{3,1},{4,6},{7,5},{8,10},{11,9},{12,14},{15,13},{16,18},{19,... | collective-permute-start | bytes 884744 | tf_op jit(solution)/shard_map/ppermute | solution.py:36
  30.7 1.5 %collective-permute-start.12 = (bf16[192,768]{1,0:T(8,128)(2,1)S(1)}, bf16[192,768]{1,0:T(8,128)(2,1)}, u32[]{:S(2)}, u32[]{:S(2)}) collective-permute-start(bf16[192,768]{1,0:T(8,128)(2,1)S(1)} %bitcast.116), channel_id=1, source_target_pairs={{1,2},{2,1},{5,6},{6,5},{9,10},{10,9},{13,14},{14,13},{17,18},{18,... | collective-permute-start | bytes 884744 | tf_op jit(solution)/shard_map/ppermute | solution.py:36
  32.2 6.6 %collective-permute-start.13 = (bf16[192,768]{1,0:T(8,128)(2,1)S(1)}, bf16[192,768]{1,0:T(8,128)(2,1)}, u32[]{:S(2)}, u32[]{:S(2)}) collective-permute-start(bf16[192,768]{1,0:T(8,128)(2,1)S(1)} %bitcast.117), channel_id=1, source_target_pairs={{0,2},{3,1},{4,6},{7,5},{8,10},{11,9},{12,14},{15,13},{16,18},{19,... | collective-permute-start | bytes 884744 | tf_op jit(solution)/shard_map/ppermute | solution.py:36
  41.5 1.6 %slice_bitcast_fusion = (bf16[768,768]{1,0:T(8,128)(2,1)}, bf16[768,768]{1,0:T(8,128)(2,1)}) fusion(bf16[2,768,768]{2,1,0:T(8,128)(2,1)S(1)} %copy-done.5), kind=kLoop, calls=%fused_computation.18 | loop fusion | bytes 4718592 | tf_op jit(solution)/shard_map/squeeze | solution.py:232
  43.1 3.3 %all-to-all-start.1 = ((f32[8,1,128]{2,1,0:T(1,128)}), f32[8,1,128]{2,1,0:T(1,128)S(1)}, u32[]{:S(2)}, u32[]{:S(2)}) async-start(f32[8,1,128]{2,1,0:T(1,128)} %bitcast.9), calls=%async_computation.1 | async-start | bytes 8192 | tf_op jit(solution)/shard_map/all_to_all | solution.py:206
  46.6 4.4 %all-to-all-done.1 = f32[8,1,128]{2,1,0:T(1,128)S(1)} async-done(((f32[8,1,128]{2,1,0:T(1,128)}), f32[8,1,128]{2,1,0:T(1,128)S(1)}, u32[]{:S(2)}, u32[]{:S(2)}) %all-to-all-start.1) | async-done | bytes 4128 | tf_op jit(solution)/shard_map/all_to_all | solution.py:206
  52.4 8.0 %collective-permute-start.11 = (bf16[192,768]{1,0:T(8,128)(2,1)S(1)}, bf16[192,768]{1,0:T(8,128)(2,1)}, u32[]{:S(2)}, u32[]{:S(2)}) collective-permute-start(bf16[192,768]{1,0:T(8,128)(2,1)S(1)} %bitcast.118), channel_id=1, source_target_pairs={{0,1},{1,0},{2,3},{3,2},{4,5},{5,4},{6,7},{7,6},{8,9},{9,8},{10,11... | collective-permute-start | bytes 884744 | tf_op jit(solution)/shard_map/ppermute | solution.py:36
  63.0 3.6 %turn_own.2 = (f32[192,768]{1,0:T(8,128)}, bf16[768,768]{1,0:T(8,128)(2,1)}) custom-call(s32[4]{0:T(128)} %pad_add_fusion.ids, bf16[192,768]{1,0:T(8,128)(2,1)} %bitcast.111, bf16[192,768]{1,0:T(8,128)(2,1)} %collective-permute-done.2.pair, bf16[192,768]{1,0:T(8,128)(2,1)} %collective-permute-done.3.near, bf16[192,768]{1,0:T(8,128)(2,1)} %collective-permute-done.4.far, ...), custom_call_target="tpu_custom_call" | custom-call | tf_op jit(solution)/shard_map/turn_own/pallas_call | solution.py:106
  66.6 2.1 %convolution_convert_fusion.1.back = bf16[192,768]{1,0:T(8,128)(2,1)S(1)} fusion(f32[2,768,192]{1,2,0:T(8,128)} %param.14, f32[192,768]{1,0:T(8,128)} %get-tuple-element.25, f32[]{:T(128)S(6)} %min_shard_map.3, f32[2,768,192]{1,2,0:T(8,128)} %param.15, bf16[2,768,768]{2,1,0:T(8,128)(2,1)S(1)} %copy-done.5), kind=kOutput, calls=%fused_computation.13 | convolution fusion | flops 228261888 | bytes 3244036 | tf_op jit(solution)/shard_map/dot_general | solution.py:19
  68.7 6.7 %collective-permute-start.7 = (bf16[192,768]{1,0:T(8,128)(2,1)S(1)}, bf16[192,768]{1,0:T(8,128)(2,1)}, u32[]{:S(2)}, u32[]{:S(2)}) collective-permute-start(bf16[192,768]{1,0:T(8,128)(2,1)S(1)} %convolution_convert_fusion.1.back), channel_id=1, source_target_pairs={{0,1},{3,2},{4,5},{7,6},{8,9},{11,10},{12,13},{15,14},{16,17},{19,... | collective-permute-start | bytes 884744 | tf_op jit(solution)/shard_map/ppermute | solution.py:36
  76.8 3.3 %collective-permute-done.15.passed_far = bf16[192,768]{1,0:T(8,128)(2,1)} collective-permute-done((bf16[192,768]{1,0:T(8,128)(2,1)}, bf16[192,768]{1,0:T(8,128)(2,1)}, u32[]{:S(2)}, u32[]{:S(2)}) %collective-permute-start.15) | collective-permute-done | bytes 294944 | tf_op jit(solution)/shard_map/ppermute | solution.py:36
  80.1 3.6 %turn_own.3 = (f32[192,768]{1,0:T(8,128)}, bf16[768,768]{1,0:T(8,128)(2,1)}) custom-call(s32[4]{0:T(128)} %pad_add_fusion.ids, bf16[192,768]{1,0:T(8,128)(2,1)} %bitcast.119, bf16[192,768]{1,0:T(8,128)(2,1)} %collective-permute-done.11.pair, bf16[192,768]{1,0:T(8,128)(2,1)} %collective-permute-done.12.near, bf16[192,768]{1,0:T(8,128)(2,1)} %collective-permute-done.13.far, ...), custom_call_target="tpu_custom_call" | custom-call | tf_op jit(solution)/shard_map/turn_own/pallas_call | solution.py:106
  83.7 2.3 %convolution_convert_fusion.back = bf16[192,768]{1,0:T(8,128)(2,1)S(1)} fusion(f32[2,768,192]{1,2,0:T(8,128)} %param.14, f32[192,768]{1,0:T(8,128)} %get-tuple-element.27, f32[]{:T(128)S(6)} %min_shard_map.3, f32[2,768,192]{1,2,0:T(8,128)} %param.15, bf16[2,768,768]{2,1,0:T(8,128)(2,1)S(1)} %copy-done.5), kind=kOutput, calls=%fused_computation.12 | convolution fusion | flops 228261888 | bytes 3244036 | tf_op jit(solution)/shard_map/dot_general | solution.py:19
  86.0 1.5 collective-permute-start.16
  88.2 4.0 %collective-permute-start.18 = (bf16[192,768]{1,0:T(8,128)(2,1)S(1)}, bf16[192,768]{1,0:T(8,128)(2,1)S(1)}, u32[]{:S(2)}, u32[]{:S(2)}) collective-permute-start(bf16[192,768]{1,0:T(8,128)(2,1)S(1)} %convolution_convert_fusion.back), channel_id=1, source_target_pairs={{0,2},{3,1},{4,6},{7,5},{8,10},{11,9},{12,14},{15,13},{16,18},{19,... | collective-permute-start | bytes 884744 | tf_op jit(solution)/shard_map/ppermute | solution.py:36
  99.2 1.7 %collective-permute-done.18.far = bf16[192,768]{1,0:T(8,128)(2,1)S(1)} collective-permute-done((bf16[192,768]{1,0:T(8,128)(2,1)S(1)}, bf16[192,768]{1,0:T(8,128)(2,1)S(1)}, u32[]{:S(2)}, u32[]{:S(2)}) %collective-permute-start.18) | collective-permute-done | bytes 294944 | tf_op jit(solution)/shard_map/ppermute | solution.py:36
  101.6 2.5 %update_both.1 = (bf16[192,768]{1,0:T(8,128)(2,1)}, bf16[192,768]{1,0:T(8,128)(2,1)}) custom-call(s32[4]{0:T(128)} %pad_add_fusion.ids, bf16[192,768]{1,0:T(8,128)(2,1)} %copy-done.11, bf16[192,768]{1,0:T(8,128)(2,1)} %copy-done.12, bf16[192,768]{1,0:T(8,128)(2,1)} %copy-done.13, bf16[192,768]{1,0:T(8,128)(2,1)} %copy-done.14, ...), custom_call_target="tpu_custom_call" | custom-call | tf_op jit(solution)/shard_map/update_both/pallas_call | solution.py:154
  105.4 2.3 %fusion.15 = (f32[1,768,192]{1,2,0:T(8,128)S(1)}, f32[1,768,192]{1,2,0:T(8,128)S(1)}, f32[1,768,192]{1,2,0:T(8,128)S(1)}, f32[1,768,192]{1,2,0:T(8,128)S(1)}) fusion(f32[192,768]{1,0:T(8,128)} %get-tuple-element.27, f32[]{:T(128)S(6)} %min_shard_map.3, f32[2,768,192]{1,2,0:T(8,128)} %param.14, f32[192,768]{1,0:T(8,128)} %get-tuple-element.25, ...), kind=kLoop, calls=%fused_computation.37 | loop fusion | flops 2359296 | bytes 5898244 | tf_op jit(solution)/shard_map/stack | solution.py:277
  108.4 2.4 %update_pair.1 = bf16[192,768]{1,0:T(8,128)(2,1)} custom-call(s32[4]{0:T(128)} %pad_add_fusion.ids, bf16[192,768]{1,0:T(8,128)(2,1)} %copy-done.8, bf16[192,768]{1,0:T(8,128)(2,1)} %collective-permute-done.7.pair, bf16[192,768]{1,0:T(8,128)(2,1)} %collective-permute-done.8.near, bf16[192,768]{1,0:T(8,128)(2,1)} %copy-done.10, ...), custom_call_target="tpu_custom_call" | custom-call | tf_op jit(solution)/shard_map/update_pair/pallas_call | solution.py:130
  112.1 8.8 %collective-permute-done.19 = bf16[192,768]{1,0:T(8,128)(2,1)} collective-permute-done((bf16[192,768]{1,0:T(8,128)(2,1)}, bf16[192,768]{1,0:T(8,128)(2,1)}, u32[]{:S(2)}, u32[]{:S(2)}) %collective-permute-start.19) | collective-permute-done | bytes 294944 | tf_op jit(solution)/shard_map/ppermute | solution.py:36
  122.8 3.5 %all-to-all-start.3 = ((bf16[8,96,192]{2,1,0:T(8,128)(2,1)}), bf16[8,96,192]{2,1,0:T(8,128)(2,1)S(1)}, u32[]{:S(2)}, u32[]{:S(2)}) async-start(bf16[8,96,192]{2,1,0:T(8,128)(2,1)} %bitcast.113), calls=%async_computation.3 | async-start | bytes 786432 | tf_op jit(solution)/shard_map/all_to_all | solution.py:262
  126.2 2.2 %pad_maximum_fusion.1 = f32[2,768,192]{1,2,0:T(8,128)} fusion(f32[1,768,192]{1,2,0:T(8,128)} %fusion.7, f32[1,768,192]{1,2,0:T(8,128)S(1)} %fusion.5), kind=kLoop, calls=%fused_computation.15 | loop fusion | flops 294912 | bytes 2359296 | tf_op jit(solution)/shard_map/stack | solution.py:276
  128.4 2.4 %update_own.1 = bf16[192,768]{1,0:T(8,128)(2,1)} custom-call(s32[4]{0:T(128)} %pad_add_fusion.ids, bf16[192,768]{1,0:T(8,128)(2,1)} %copy-done.8, bf16[192,768]{1,0:T(8,128)(2,1)} %collective-permute-done.7.pair, bf16[192,768]{1,0:T(8,128)(2,1)} %collective-permute-done.8.near, bf16[192,768]{1,0:T(8,128)(2,1)} %copy-done.10, ...), custom_call_target="tpu_custom_call" | custom-call | tf_op jit(solution)/shard_map/update_own/pallas_call | solution.py:130
  132.7 1.8 %all-to-all-done.3.returned = bf16[8,96,192]{2,1,0:T(8,128)(2,1)S(1)} async-done(((bf16[8,96,192]{2,1,0:T(8,128)(2,1)}), bf16[8,96,192]{2,1,0:T(8,128)(2,1)S(1)}, u32[]{:S(2)}, u32[]{:S(2)}) %all-to-all-start.3) | async-done | bytes 294944 | tf_op jit(solution)/shard_map/all_to_all | solution.py:262
  134.5 3.5 %all-to-all-start.2 = ((bf16[8,96,192]{2,1,0:T(8,128)(2,1)}), bf16[8,96,192]{2,1,0:T(8,128)(2,1)S(1)}, u32[]{:S(2)}, u32[]{:S(2)}) async-start(bf16[8,96,192]{2,1,0:T(8,128)(2,1)} %bitcast.114), calls=%async_computation.2 | async-start | bytes 786432 | tf_op jit(solution)/shard_map/all_to_all | solution.py:262
  141.5 4.7 %all-to-all-done.2.returned = bf16[8,96,192]{2,1,0:T(8,128)(2,1)S(1)} async-done(((bf16[8,96,192]{2,1,0:T(8,128)(2,1)}), bf16[8,96,192]{2,1,0:T(8,128)(2,1)S(1)}, u32[]{:S(2)}, u32[]{:S(2)}) %all-to-all-start.2) | async-done | bytes 294944 | tf_op jit(solution)/shard_map/all_to_all | solution.py:262
  (85 shorter events, 35.0 us)
Async XLA Ops:
  0.6 9.3 %copy-start.4 = (bf16[2,768,768]{2,1,0:T(8,128)(2,1)S(1)}, bf16[2,768,768]{2,1,0:T(8,128)(2,1)}, u32[]{:S(2)}) copy-start(bf16[2,768,768]{2,1,0:T(8,128)(2,1)} %param.13) | copy-start | bytes 7077892
  3.0 17.9 %all-to-all-start = ((bf16[8,192,192]{2,1,0:T(8,128)(2,1)}), bf16[8,192,192]{2,1,0:T(8,128)(2,1)S(1)}, u32[]{:S(2)}, u32[]{:S(2)}) async-start(bf16[8,192,192]{2,1,0:T(8,128)(2,1)} %get-tuple-element.19), calls=%async_computation | async-start | bytes 1572864 | tf_op jit(solution)/shard_map/all_to_all | solution.py:203
  8.3 4.6 %collective-permute-start = (f32[8,128]{1,0:T(8,128)S(1)}, f32[8,128]{1,0:T(8,128)S(1)}, u32[]{:S(2)}, u32[]{:S(2)}) collective-permute-start(f32[8,128]{1,0:T(8,128)S(1)} %copy-done.15), channel_id=1, source_target_pairs={{0,1},{1,0},{2,3},{3,2},{4,5},{5,4},{6,7},{7,6},{8,9},{9,8},{10,11... | collective-permute-start | bytes 12296 | tf_op jit(solution)/shard_map/ppermute | solution.py:30
  12.9 4.5 %collective-permute-start.1 = (f32[8,128]{1,0:T(8,128)S(1)}, f32[8,128]{1,0:T(8,128)S(1)}, u32[]{:S(2)}, u32[]{:S(2)}) collective-permute-start(f32[8,128]{1,0:T(8,128)S(1)} %add.46), channel_id=1, source_target_pairs={{0,2},{1,3},{2,0},{3,1},{4,6},{5,7},{6,4},{7,5},{8,10},{9,11},{10,... | collective-permute-start | bytes 12296 | tf_op jit(solution)/shard_map/ppermute | solution.py:30
  20.9 20.6 %copy-start.5 = (bf16[2,768,768]{2,1,0:T(8,128)(2,1)S(1)}, bf16[2,768,768]{2,1,0:T(8,128)(2,1)}, u32[]{:S(2)}) copy-start(bf16[2,768,768]{2,1,0:T(8,128)(2,1)} %param.12) | copy-start | bytes 7077892
  22.9 20.1 %copy-start.2 = (bf16[768,192]{0,1:T(8,128)(2,1)}, bf16[768,192]{0,1:T(8,128)(2,1)S(1)}, u32[]{:S(2)}) copy-start(bf16[768,192]{0,1:T(8,128)(2,1)S(1)} %copy.28) | copy-start | bytes 884740
  22.9 15.9 %collective-permute-start.3 = (bf16[192,768]{1,0:T(8,128)(2,1)S(1)}, bf16[192,768]{1,0:T(8,128)(2,1)}, u32[]{:S(2)}, u32[]{:S(2)}) collective-permute-start(bf16[192,768]{1,0:T(8,128)(2,1)S(1)} %bitcast.108), channel_id=1, source_target_pairs={{1,2},{2,1},{5,6},{6,5},{9,10},{10,9},{13,14},{14,13},{17,18},{18,... | collective-permute-start | bytes 884744 | tf_op jit(solution)/shard_map/ppermute | solution.py:36
  24.3 15.9 %collective-permute-start.4 = (bf16[192,768]{1,0:T(8,128)(2,1)S(1)}, bf16[192,768]{1,0:T(8,128)(2,1)}, u32[]{:S(2)}, u32[]{:S(2)}) collective-permute-start(bf16[192,768]{1,0:T(8,128)(2,1)S(1)} %bitcast.109), channel_id=1, source_target_pairs={{0,2},{3,1},{4,6},{7,5},{8,10},{11,9},{12,14},{15,13},{16,18},{19,... | collective-permute-start | bytes 884744 | tf_op jit(solution)/shard_map/ppermute | solution.py:36
  30.5 21.9 %collective-permute-start.2 = (bf16[192,768]{1,0:T(8,128)(2,1)S(1)}, bf16[192,768]{1,0:T(8,128)(2,1)}, u32[]{:S(2)}, u32[]{:S(2)}) collective-permute-start(bf16[192,768]{1,0:T(8,128)(2,1)S(1)} %bitcast.110), channel_id=1, source_target_pairs={{0,1},{1,0},{2,3},{3,2},{4,5},{5,4},{6,7},{7,6},{8,9},{9,8},{10,11... | collective-permute-start | bytes 884744 | tf_op jit(solution)/shard_map/ppermute | solution.py:36
  30.7 21.7 %copy-start.9 = (bf16[768,192]{0,1:T(8,128)(2,1)}, bf16[768,192]{0,1:T(8,128)(2,1)S(1)}, u32[]{:S(2)}) copy-start(bf16[768,192]{0,1:T(8,128)(2,1)S(1)} %copy.29) | copy-start | bytes 884740
  30.7 12.3 %copy-start.16 = (s32[16]{0:T(128)S(1)}, s32[16]{0:T(128)}, u32[]{:S(2)}) copy-start(s32[16]{0:T(128)} %slots.1) | copy-start | bytes 196
  30.7 29.7 %collective-permute-start.12 = (bf16[192,768]{1,0:T(8,128)(2,1)S(1)}, bf16[192,768]{1,0:T(8,128)(2,1)}, u32[]{:S(2)}, u32[]{:S(2)}) collective-permute-start(bf16[192,768]{1,0:T(8,128)(2,1)S(1)} %bitcast.116), channel_id=1, source_target_pairs={{1,2},{2,1},{5,6},{6,5},{9,10},{10,9},{13,14},{14,13},{17,18},{18,... | collective-permute-start | bytes 884744 | tf_op jit(solution)/shard_map/ppermute | solution.py:36
  32.2 29.4 %collective-permute-start.13 = (bf16[192,768]{1,0:T(8,128)(2,1)S(1)}, bf16[192,768]{1,0:T(8,128)(2,1)}, u32[]{:S(2)}, u32[]{:S(2)}) collective-permute-start(bf16[192,768]{1,0:T(8,128)(2,1)S(1)} %bitcast.117), channel_id=1, source_target_pairs={{0,2},{3,1},{4,6},{7,5},{8,10},{11,9},{12,14},{15,13},{16,18},{19,... | collective-permute-start | bytes 884744 | tf_op jit(solution)/shard_map/ppermute | solution.py:36
  38.8 24.1 %collective-permute-start.5 = (bf16[192,768]{1,0:T(8,128)(2,1)}, bf16[192,768]{1,0:T(8,128)(2,1)}, u32[]{:S(2)}, u32[]{:S(2)}) collective-permute-start(bf16[192,768]{1,0:T(8,128)(2,1)} %collective-permute-done.3.near), channel_id=1, source_target_pairs={{1,0},{2,3},{5,4},{6,7},{9,8},{10,11},{13,12},{14,15},{17,16},{18,... | collective-permute-start | bytes 884744 | tf_op jit(solution)/shard_map/ppermute | solution.py:36
  40.1 22.8 %collective-permute-start.6 = (bf16[192,768]{1,0:T(8,128)(2,1)}, bf16[192,768]{1,0:T(8,128)(2,1)}, u32[]{:S(2)}, u32[]{:S(2)}) collective-permute-start(bf16[192,768]{1,0:T(8,128)(2,1)} %collective-permute-done.4.far), channel_id=1, source_target_pairs={{1,0},{2,3},{5,4},{6,7},{9,8},{10,11},{13,12},{14,15},{17,16},{18,... | collective-permute-start | bytes 884744 | tf_op jit(solution)/shard_map/ppermute | solution.py:36
  43.1 7.9 %all-to-all-start.1 = ((f32[8,1,128]{2,1,0:T(1,128)}), f32[8,1,128]{2,1,0:T(1,128)S(1)}, u32[]{:S(2)}, u32[]{:S(2)}) async-start(f32[8,1,128]{2,1,0:T(1,128)} %bitcast.9), calls=%async_computation.1 | async-start | bytes 8192 | tf_op jit(solution)/shard_map/all_to_all | solution.py:206
  52.4 24.4 %collective-permute-start.11 = (bf16[192,768]{1,0:T(8,128)(2,1)S(1)}, bf16[192,768]{1,0:T(8,128)(2,1)}, u32[]{:S(2)}, u32[]{:S(2)}) collective-permute-start(bf16[192,768]{1,0:T(8,128)(2,1)S(1)} %bitcast.118), channel_id=1, source_target_pairs={{0,1},{1,0},{2,3},{3,2},{4,5},{5,4},{6,7},{7,6},{8,9},{9,8},{10,11... | collective-permute-start | bytes 884744 | tf_op jit(solution)/shard_map/ppermute | solution.py:36
  60.3 16.4 %collective-permute-start.14 = (bf16[192,768]{1,0:T(8,128)(2,1)}, bf16[192,768]{1,0:T(8,128)(2,1)}, u32[]{:S(2)}, u32[]{:S(2)}) collective-permute-start(bf16[192,768]{1,0:T(8,128)(2,1)} %collective-permute-done.12.near), channel_id=1, source_target_pairs={{1,0},{2,3},{5,4},{6,7},{9,8},{10,11},{13,12},{14,15},{17,16},{18,... | collective-permute-start | bytes 884744 | tf_op jit(solution)/shard_map/ppermute | solution.py:36
  61.6 18.4 %collective-permute-start.15 = (bf16[192,768]{1,0:T(8,128)(2,1)}, bf16[192,768]{1,0:T(8,128)(2,1)}, u32[]{:S(2)}, u32[]{:S(2)}) collective-permute-start(bf16[192,768]{1,0:T(8,128)(2,1)} %collective-permute-done.13.far), channel_id=1, source_target_pairs={{1,0},{2,3},{5,4},{6,7},{9,8},{10,11},{13,12},{14,15},{17,16},{18,... | collective-permute-start | bytes 884744 | tf_op jit(solution)/shard_map/ppermute | solution.py:36
  68.7 29.1 %copy-start.8 = (bf16[192,768]{1,0:T(8,128)(2,1)}, bf16[192,768]{1,0:T(8,128)(2,1)S(1)}, u32[]{:S(2)}) copy-start(bf16[192,768]{1,0:T(8,128)(2,1)S(1)} %convolution_convert_fusion.1.back) | copy-start | bytes 884740
  68.7 39.0 %collective-permute-start.7 = (bf16[192,768]{1,0:T(8,128)(2,1)S(1)}, bf16[192,768]{1,0:T(8,128)(2,1)}, u32[]{:S(2)}, u32[]{:S(2)}) collective-permute-start(bf16[192,768]{1,0:T(8,128)(2,1)S(1)} %convolution_convert_fusion.1.back), channel_id=1, source_target_pairs={{0,1},{3,2},{4,5},{7,6},{8,9},{11,10},{12,13},{15,14},{16,17},{19,... | collective-permute-start | bytes 884744 | tf_op jit(solution)/shard_map/ppermute | solution.py:36
  75.4 32.3 %collective-permute-start.8 = (bf16[192,768]{1,0:T(8,128)(2,1)S(1)}, bf16[192,768]{1,0:T(8,128)(2,1)}, u32[]{:S(2)}, u32[]{:S(2)}) collective-permute-start(bf16[192,768]{1,0:T(8,128)(2,1)S(1)} %convolution_convert_fusion.1.back), channel_id=1, source_target_pairs={{1,2},{2,1},{5,6},{6,5},{9,10},{10,9},{13,14},{14,13},{17,18},{18,... | collective-permute-start | bytes 884744 | tf_op jit(solution)/shard_map/ppermute | solution.py:36
  83.7 8.5 %copy-start = (bf16[768,768]{1,0:T(8,128)(2,1)S(1)}, bf16[768,768]{1,0:T(8,128)(2,1)}, u32[]{:S(2)}) copy-start(bf16[768,768]{1,0:T(8,128)(2,1)} %get-tuple-element.31) | copy-start | bytes 3538948
  83.7 8.5 %copy-start.6 = (f32[2,768,192]{1,2,0:T(8,128)S(1)}, f32[2,768,192]{1,2,0:T(8,128)}, u32[]{:S(2)}) copy-start(f32[2,768,192]{1,2,0:T(8,128)} %param.10) | copy-start | bytes 3538948
  86.0 11.8 %collective-permute-start.16 = (bf16[192,768]{1,0:T(8,128)(2,1)S(1)}, bf16[192,768]{1,0:T(8,128)(2,1)S(1)}, u32[]{:S(2)}, u32[]{:S(2)}) collective-permute-start(bf16[192,768]{1,0:T(8,128)(2,1)S(1)} %convolution_convert_fusion.back), channel_id=1, source_target_pairs={{0,1},{3,2},{4,5},{7,6},{8,9},{11,10},{12,13},{15,14},{16,17},{19,... | collective-permute-start | bytes 884744 | tf_op jit(solution)/shard_map/ppermute | solution.py:36
  87.5 11.7 %collective-permute-start.17 = (bf16[192,768]{1,0:T(8,128)(2,1)S(1)}, bf16[192,768]{1,0:T(8,128)(2,1)S(1)}, u32[]{:S(2)}, u32[]{:S(2)}) collective-permute-start(bf16[192,768]{1,0:T(8,128)(2,1)S(1)} %convolution_convert_fusion.back), channel_id=1, source_target_pairs={{1,2},{2,1},{5,6},{6,5},{9,10},{10,9},{13,14},{14,13},{17,18},{18,... | collective-permute-start | bytes 884744 | tf_op jit(solution)/shard_map/ppermute | solution.py:36
  88.2 12.7 %collective-permute-start.18 = (bf16[192,768]{1,0:T(8,128)(2,1)S(1)}, bf16[192,768]{1,0:T(8,128)(2,1)S(1)}, u32[]{:S(2)}, u32[]{:S(2)}) collective-permute-start(bf16[192,768]{1,0:T(8,128)(2,1)S(1)} %convolution_convert_fusion.back), channel_id=1, source_target_pairs={{0,2},{3,1},{4,6},{7,5},{8,10},{11,9},{12,14},{15,13},{16,18},{19,... | collective-permute-start | bytes 884744 | tf_op jit(solution)/shard_map/ppermute | solution.py:36
  97.8 9.9 %collective-permute-start.9 = (bf16[192,768]{1,0:T(8,128)(2,1)S(1)}, bf16[192,768]{1,0:T(8,128)(2,1)S(1)}, u32[]{:S(2)}, u32[]{:S(2)}) collective-permute-start(bf16[192,768]{1,0:T(8,128)(2,1)S(1)} %convolution_convert_fusion.1.back), channel_id=1, source_target_pairs={{0,2},{3,1},{4,6},{7,5},{8,10},{11,9},{12,14},{15,13},{16,18},{19,... | collective-permute-start | bytes 884744 | tf_op jit(solution)/shard_map/ppermute | solution.py:36
  104.1 16.8 %collective-permute-start.19 = (bf16[192,768]{1,0:T(8,128)(2,1)}, bf16[192,768]{1,0:T(8,128)(2,1)}, u32[]{:S(2)}, u32[]{:S(2)}) collective-permute-start(bf16[192,768]{1,0:T(8,128)(2,1)} %get-tuple-element.28), channel_id=1, source_target_pairs={{1,0},{2,3},{5,4},{6,7},{9,8},{10,11},{13,12},{14,15},{17,16},{18,... | collective-permute-start | bytes 884744 | tf_op jit(solution)/shard_map/ppermute | solution.py:36
  110.8 20.0 %collective-permute-start.10 = (bf16[192,768]{1,0:T(8,128)(2,1)}, bf16[192,768]{1,0:T(8,128)(2,1)}, u32[]{:S(2)}, u32[]{:S(2)}) collective-permute-start(bf16[192,768]{1,0:T(8,128)(2,1)} %update_pair.1), channel_id=1, source_target_pairs={{1,0},{2,3},{5,4},{6,7},{9,8},{10,11},{13,12},{14,15},{17,16},{18,... | collective-permute-start | bytes 884744 | tf_op jit(solution)/shard_map/ppermute | solution.py:36
  122.8 11.7 %all-to-all-start.3 = ((bf16[8,96,192]{2,1,0:T(8,128)(2,1)}), bf16[8,96,192]{2,1,0:T(8,128)(2,1)S(1)}, u32[]{:S(2)}, u32[]{:S(2)}) async-start(bf16[8,96,192]{2,1,0:T(8,128)(2,1)} %bitcast.113), calls=%async_computation.3 | async-start | bytes 786432 | tf_op jit(solution)/shard_map/all_to_all | solution.py:262
  134.5 11.7 %all-to-all-start.2 = ((bf16[8,96,192]{2,1,0:T(8,128)(2,1)}), bf16[8,96,192]{2,1,0:T(8,128)(2,1)S(1)}, u32[]{:S(2)}, u32[]{:S(2)}) async-start(bf16[8,96,192]{2,1,0:T(8,128)(2,1)} %bitcast.114), calls=%async_computation.2 | async-start | bytes 786432 | tf_op jit(solution)/shard_map/all_to_all | solution.py:262
  (9 other events, 22.1 us)
